TPU v7x, 32 devices: a whole 2x2x4 slice. The times are simulated.
32 devices in a mesh: chan: 16 (over z, y, core), dist: 2 (over x).
Axes of the slice: x: 2, y: 2, z: 4, core: 2. Of those that a mesh axis runs over, the one named last changes fastest.
Arguments:
- q_now: float32 [16384, 256], P('chan', 'dist'), may hold values from -6 to 6
- q_prev: float32 [16384, 256], P('chan', 'dist'), may hold values from -6 to 6
- panels: bfloat16 [4, 16384, 2048], P(None, 'chan'), may hold values from -0.0625 to 0.0625
- col_block: int32 [16, 4], P('chan'), may hold values from 0 to 7, as said below
- lam_index: int32 [16, 4], P('chan'), may hold values from 0 to 7
- energies: float32 [16384], P('chan'), may hold values from -0.4 to 0.4
- radial: float32 [8, 256], P(None, 'dist'), may hold values from -2 to 2
- damping: float32 [256], P('dist'), may hold values from 0.5 to 1
Outputs:
- q_out: float32 [16384, 256], P('chan', 'dist')
- q_last: float32 [16384, 256], P('chan', 'dist')
Inputs may be any that keep to these rules, and one draw needn't show every extreme that they name: `col_block`: each row names 4 different column blocks.
All inputs are finite; a program needn't handle non-finite values.
Results may differ from a plain program's by a relative error of at most 0.0027.
Values may be sent and summed in bfloat16 or wider, within the bound.
No kernel may reach another device: no remote copies, remote signals or barrier semaphores. Data moves between devices by JAX's collectives and lax.ppermute only.
A program may use at most 64 MiB of HBM per device.

v0:
```python
import jax
import jax.numpy as jnp
import numpy as np
from jax import lax
from jax.experimental import pallas as pl
from jax.experimental.pallas import tpu as pltpu
from jax.sharding import PartitionSpec as P


KCHEB = 3
NR = 8
CORES = 2

stencil = (
    -1.0 / 560.0,
    8.0 / 315.0,
    -0.2,
    1.6,
    -205.0 / 72.0,
    1.6,
    -0.2,
    8.0 / 315.0,
    -1.0 / 560.0,
)
kinetic_scale = 0.04


def ring_order(chips):
    return list(range(0, chips, 2)) + list(range(1, chips, 2))[::-1]


def ring_perm(chips):
    order = ring_order(chips)
    perm = []
    for at in range(chips):
        perm.append((CORES * order[at], CORES * order[(at + 1) % chips]))
        perm.append((CORES * order[at] + 1, CORES * order[(at - 1) % chips] + 1))
    return perm


def chip_at(place, chips):
    half = (chips + 1) // 2
    place = lax.rem(place + 2 * chips, chips)
    return jnp.where(place < half, 2 * place, 2 * (chips - 1 - place) + 1)


def place_of(chip, chips):
    return jnp.where(lax.rem(chip, 2) == 0, lax.div(chip, 2), chips - 1 - lax.div(chip, 2))


def stencil_matrices(points):
    wide = np.zeros((3 * points, points), np.float64)
    for point in range(points):
        for tap, scale in enumerate(stencil):
            scale = -2.0 * kinetic_scale * scale
            wide[points + point + (tap - 4) * NR, point] += scale
            small = point % NR + tap - 4
            if 0 <= small < NR:
                wide[points + point + tap - 4, point] += scale
    mats = np.stack([wide[points : 2 * points], wide[:points], wide[2 * points :]]).astype(np.float32)
    high = mats.astype(jnp.bfloat16)
    low = (mats - high.astype(np.float32)).astype(jnp.bfloat16)
    return jnp.asarray(np.stack([high, low]))


def vmem(x):
    return pltpu.with_memory_space_constraint(x, pltpu.VMEM)


VSPEC = pl.BlockSpec(memory_space=pltpu.VMEM)
SSPEC = pl.BlockSpec(memory_space=pltpu.SMEM)
VMEM_BYTES = 12 << 20
OWN, RING, SWAP = 0, -1, 1


def prepare(q_now, where):
    def kernel(where, x, out):
        out[...] = x[...].astype(jnp.bfloat16)

    return pl.pallas_call(
        kernel,
        out_shape=pltpu.VMEM(q_now.shape, jnp.bfloat16),
        in_specs=[SSPEC, VSPEC],
        out_specs=VSPEC,
        cost_estimate=pl.CostEstimate(flops=12 * 10**9, transcendentals=0, bytes_accessed=q_now.size * 6),
        compiler_params=pltpu.CompilerParams(vmem_limit_bytes=VMEM_BYTES),
        name="prepare",
    )(where, q_now)


class Stages:
    def __init__(self, chips, shape, panels, nbrs, common):
        self.chips = chips
        self.rows, self.points = shape
        self.panels_n, _, self.cols = panels.shape
        self.nbrs = nbrs
        self.common = common

    def run(self, parts, acc=None, base=(), out="acc"):
        rows, points, cols, chips = self.rows, self.points, self.cols, self.chips
        chips_per_block = cols // (CORES * rows)
        first = acc is None
        counts = [len(shards) for _, _, shards in parts]

        def kernel(where, col, lam, panels, radial, damp, *refs):
            refs = list(refs)
            shards = [[refs.pop(0) for _ in range(n)] for n in counts]
            terms = [refs.pop(0) for _ in base]
            old = None if first else refs.pop(0)
            new = refs.pop(0)
            rounded = refs.pop(0) if out == "both" else None
            me = where[0]
            core = lax.rem(me, CORES)
            place = place_of(lax.div(me, CORES), chips)
            way = 1 - 2 * core
            scale = damp[...]

            def write(value):
                new[...] = value
                if rounded is not None:
                    rounded[...] = value.astype(jnp.bfloat16)

            if first:
                new[...] = jnp.zeros_like(new)

            if base:
                cur, before, energy, mats = terms[:4]
                own = cur[...]
                values = [own] + [side[...] for side in terms[4:]]
                highs = [v.astype(jnp.bfloat16) for v in values]
                lows = [(v - h.astype(jnp.float32)).astype(jnp.bfloat16) for v, h in zip(values, highs)]
                if self.nbrs == 1:
                    picks = [0, jnp.where(where[1] == 0, 2, 1)]
                else:
                    picks = list(range(len(values)))
                join = lambda xs, axis: jnp.concatenate(xs, axis=axis) if len(xs) > 1 else xs[0]
                mat = [join([mats[i, at] for at in picks], 0) for i in range(2)]
                high, low = join(highs, 1), join(lows, 1)
                dot = lambda a, b: jnp.dot(a, b, preferred_element_type=jnp.float32)
                total = dot(high, mat[0]) + dot(low, mat[0]) + dot(high, mat[1])
                new[...] = old[...] + scale * (total + 2.0 * energy[...] * own - scale * before[...])
                old = new

            for at, ((side, distance, described), shard_refs) in enumerate(zip(parts, shards)):
                if side == OWN:
                    chip = lax.div(me, CORES)
                else:
                    chip = chip_at(place + side * way * distance, chips)
                block = lax.div(chip, chips_per_block)
                start = lax.rem(chip, chips_per_block) * (CORES * rows)
                which = jnp.int32(0)
                found = col[0, 0] == block
                for j in range(1, self.panels_n):
                    hit = col[0, j] == block
                    which = jnp.where(hit, j, which)
                    found = found | hit
                source = new if first or base or at else old

                @pl.when(found)
                def _():
                    total = None
                    for (whose, _), shard in zip(described, shard_refs):
                        of_core = core if whose == 0 else 1 - core
                        off = pl.multiple_of(start + of_core * rows, 128)
                        part = jnp.dot(panels[which, :, pl.ds(off, rows)], shard[...], preferred_element_type=jnp.float32)
                        total = part if total is None else total + part
                    weight = 2.0 * scale * radial[pl.ds(lam[0, which], 1), :]
                    value = source[...] + weight * total
                    if at == len(parts) - 1:
                        write(value)
                    else:
                        new[...] = value

                if out != "acc" and at == len(parts) - 1:

                    @pl.when(jnp.logical_not(found))
                    def _():
                        write(source[...])

        where, col, lam, panels, radial, damp = self.common
        args = [where, col, lam, vmem(panels), radial, damp]
        specs = [SSPEC] * 3 + [VSPEC] * 3
        for x in [shard for _, _, shards in parts for _, shard in shards] + list(base):
            args.append(vmem(x))
            specs.append(VSPEC)
        alias = {}
        if not first:
            if out != "final":
                alias = {len(args): 0}
            args.append(vmem(acc))
            specs.append(VSPEC)
        if out == "final":
            outs = [jax.ShapeDtypeStruct((rows, points), jnp.float32)]
        else:
            outs = [pltpu.VMEM((rows, points), jnp.float32)]
        if out == "both":
            outs.append(pltpu.VMEM((rows, points), jnp.bfloat16))
        products = sum(counts)
        done = pl.pallas_call(
            kernel,
            out_shape=outs,
            in_specs=specs,
            out_specs=[VSPEC] * len(outs),
            input_output_aliases=alias,
            cost_estimate=pl.CostEstimate(
                flops=products * rows * rows * points, transcendentals=0, bytes_accessed=rows * points * 8
            ),
            compiler_params=pltpu.CompilerParams(vmem_limit_bytes=VMEM_BYTES),
        )(*args)
        return done if len(done) > 1 else done[0]


def local(q_now, q_prev, panels, col_block, lam_index, energies, radial, damping):
    count = lax.axis_size("chan")
    dist_n = lax.axis_size("dist")
    chips = count // CORES
    far = chips // 2
    rows, points = q_now.shape
    where = jnp.stack([lax.axis_index("chan"), lax.axis_index("dist")]).astype(jnp.int32)
    ring = ring_perm(chips)
    swap = [(i, i ^ 1) for i in range(count)]
    energy = jnp.broadcast_to(energies[:, None], (rows, points))
    mats = stencil_matrices(points)
    right = [(i, i + 1) for i in range(dist_n - 1)]
    left = [(i + 1, i) for i in range(dist_n - 1)]
    if dist_n == 1:
        shifts = []
    elif dist_n == 2:
        shifts = [right + left]
    else:
        shifts = [right, left]
    common = (where, col_block, lam_index, panels, radial, damping[None, :])
    stages = Stages(chips, (rows, points), panels, len(shifts), common)

    current, before = q_now, q_prev
    rounded = prepare(q_now, where)
    for turn in range(KCHEB):
        final = turn == KCHEB - 1
        p = lax.ppermute(rounded, "chan", ring)
        partner = lax.ppermute(rounded, "chan", swap)
        sides = [lax.ppermute(current, "dist", perm) for perm in shifts]
        q = lax.ppermute(partner, "chan", ring)
        acc = stages.run([(OWN, 0, ((0, rounded), (1, partner)))])
        for r in range(1, far):
            next_p = lax.ppermute(p, "chan", ring)
            swap_p = lax.ppermute(p, "chan", swap)
            if r + 1 < far:
                next_q = lax.ppermute(q, "chan", ring)
            swap_q = lax.ppermute(q, "chan", swap)
            parts = [(RING, r, ((0, p), (1, q))), (SWAP, r, ((1, swap_p), (0, swap_q)))]
            if r + 1 == far:
                acc = stages.run([], acc, [current, before, energy, mats] + sides)
            acc = stages.run(parts, acc)
            p, q = next_p, next_q
        swap_p = lax.ppermute(p, "chan", swap)
        acc = stages.run([(RING, far, ((0, p),))], acc)
        done = stages.run([(SWAP, far, ((1, swap_p),))], acc, out="final" if final else "both")
        before = current
        if final:
            current = done
        else:
            current, rounded = done
    return (current, before)


def solution(mesh):
    return jax.shard_map(
        local,
        mesh=mesh,
        in_specs=(
            P("chan", "dist"),
            P("chan", "dist"),
            P(None, "chan", None),
            P("chan", None),
            P("chan", None),
            P("chan"),
            P(None, "dist"),
            P("dist"),
        ),
        out_specs=(P("chan", "dist"), P("chan", "dist")),
        check_vma=False,
    )
```

profile of v0, /device:TPU:0, one launch (start us, length us, event | category | flops | bytes accessed | tf_op | source)
XLA Modules:
  0.0 114.1 jit_solution(5520698704178201607)
XLA Ops:
  2.5 2.6 %collective-permute-start = (bf16[1024,128]{1,0:T(8,128)(2,1)S(1)}, bf16[1024,128]{1,0:T(8,128)(2,1)S(1)}, u32[]{:S(2)}, u32[]{:S(2)}) collective-permute-start(bf16[1024,128]{1,0:T(8,128)(2,1)S(1)} %prepare.1.refs_0_), channel_id=1, source_target_pairs={{0,8},{2,6},{8,16},{10,2},{16,24},{18,10},{24,28},{26,18},{28,20},... | collective-permute-start | bytes 786440 | tf_op jit(solution)/shard_map/ppermute | solution.py:239
  6.7 2.7 %collective-permute-done.refs_0_ = bf16[1024,128]{1,0:T(8,128)(2,1)S(1)} collective-permute-done((bf16[1024,128]{1,0:T(8,128)(2,1)S(1)}, bf16[1024,128]{1,0:T(8,128)(2,1)S(1)}, u32[]{:S(2)}, u32[]{:S(2)}) %collective-permute-start) | collective-permute-done | bytes 262176 | tf_op jit(solution)/shard_map/ppermute | solution.py:239
  9.4 2.1 %collective-permute-start.1 = (bf16[1024,128]{1,0:T(8,128)(2,1)S(1)}, bf16[1024,128]{1,0:T(8,128)(2,1)S(1)}, u32[]{:S(2)}, u32[]{:S(2)}) collective-permute-start(bf16[1024,128]{1,0:T(8,128)(2,1)S(1)} %collective-permute-done.refs_0_), channel_id=1, source_target_pairs={{0,8},{2,6},{8,16},{10,2},{16,24},{18,10},{24,28},{26,18},{28,20},... | collective-permute-start | bytes 786440 | tf_op jit(solution)/shard_map/ppermute | solution.py:245
  12.3 2.1 %collective-permute-start.7 = (bf16[1024,128]{1,0:T(8,128)(2,1)S(1)}, bf16[1024,128]{1,0:T(8,128)(2,1)S(1)}, u32[]{:S(2)}, u32[]{:S(2)}) collective-permute-start(bf16[1024,128]{1,0:T(8,128)(2,1)S(1)} %collective-permute-done.6.refs_1_), channel_id=1, source_target_pairs={{0,8},{2,6},{8,16},{10,2},{16,24},{18,10},{24,28},{26,18},{28,20},... | collective-permute-start | bytes 786440 | tf_op jit(solution)/shard_map/ppermute | solution.py:248
  15.8 2.1 %collective-permute-start.2 = (bf16[1024,128]{1,0:T(8,128)(2,1)S(1)}, bf16[1024,128]{1,0:T(8,128)(2,1)S(1)}, u32[]{:S(2)}, u32[]{:S(2)}) collective-permute-start(bf16[1024,128]{1,0:T(8,128)(2,1)S(1)} %collective-permute-done.1.refs_0_), channel_id=1, source_target_pairs={{0,8},{2,6},{8,16},{10,2},{16,24},{18,10},{24,28},{26,18},{28,20},... | collective-permute-start | bytes 786440 | tf_op jit(solution)/shard_map/ppermute | solution.py:245
  22.2 2.1 %collective-permute-start.3 = (bf16[1024,128]{1,0:T(8,128)(2,1)S(1)}, bf16[1024,128]{1,0:T(8,128)(2,1)S(1)}, u32[]{:S(2)}, u32[]{:S(2)}) collective-permute-start(bf16[1024,128]{1,0:T(8,128)(2,1)S(1)} %collective-permute-done.2.refs_0_), channel_id=1, source_target_pairs={{0,8},{2,6},{8,16},{10,2},{16,24},{18,10},{24,28},{26,18},{28,20},... | collective-permute-start | bytes 786440 | tf_op jit(solution)/shard_map/ppermute | solution.py:245
  26.0 2.8 %collective-permute-done.3.refs_0_ = bf16[1024,128]{1,0:T(8,128)(2,1)S(1)} collective-permute-done((bf16[1024,128]{1,0:T(8,128)(2,1)S(1)}, bf16[1024,128]{1,0:T(8,128)(2,1)S(1)}, u32[]{:S(2)}, u32[]{:S(2)}) %collective-permute-start.3) | collective-permute-done | bytes 262176 | tf_op jit(solution)/shard_map/ppermute | solution.py:245
  28.9 1.8 %shard_map.104.refs_4_ = f32[1024,128]{1,0:T(8,128)S(1)} custom-call(s32[2]{0:T(128)S(1)} %pad_add_fusion.where, s32[1,4]{1,0:T(1,128)S(1)} %copy-done.4, s32[1,4]{1,0:T(1,128)S(1)} %copy-done.5, bf16[4,1024,2048]{2,1,0:T(8,128)(2,1)S(1)} %copy-done, f32[8,128]{1,0:T(8,128)S(1)} %copy-done.1, f32[1,128]{1,0:T(1,128)S(1)} %bitcast.3, ...), custom_call_target="tpu_custom_call" | custom-call | flops 268435456 | bytes 1048576 | tf_op jit(solution)/shard_map/pallas_call | solution.py:199
  30.7 1.8 %shard_map.105.refs_4_ = f32[1024,128]{1,0:T(8,128)S(1)} custom-call(s32[2]{0:T(128)S(1)} %pad_add_fusion.where, s32[1,4]{1,0:T(1,128)S(1)} %copy-done.4, s32[1,4]{1,0:T(1,128)S(1)} %copy-done.5, bf16[4,1024,2048]{2,1,0:T(8,128)(2,1)S(1)} %copy-done, f32[8,128]{1,0:T(8,128)S(1)} %copy-done.1, f32[1,128]{1,0:T(1,128)S(1)} %bitcast.4, ...), custom_call_target="tpu_custom_call", output_to_operand_aliasing={{}: (10, {})} | custom-call | flops 536870912 | bytes 1048576 | tf_op jit(solution)/shard_map/pallas_call | solution.py:199
  33.4 1.7 %shard_map.107.refs_4_ = f32[1024,128]{1,0:T(8,128)S(1)} custom-call(s32[2]{0:T(128)S(1)} %pad_add_fusion.where, s32[1,4]{1,0:T(1,128)S(1)} %copy-done.4, s32[1,4]{1,0:T(1,128)S(1)} %copy-done.5, bf16[4,1024,2048]{2,1,0:T(8,128)(2,1)S(1)} %copy-done, f32[8,128]{1,0:T(8,128)S(1)} %copy-done.1, f32[1,128]{1,0:T(1,128)S(1)} %bitcast.6, ...), custom_call_target="tpu_custom_call", output_to_operand_aliasing={{}: (11, {})} | custom-call | bytes 1048576 | tf_op jit(solution)/shard_map/pallas_call | solution.py:199
  35.2 3.1 %shard_map.108.refs_1_ = f32[1024,128]{1,0:T(8,128)S(1)} custom-call(s32[2]{0:T(128)S(1)} %pad_add_fusion.where, s32[1,4]{1,0:T(1,128)S(1)} %copy-done.4, s32[1,4]{1,0:T(1,128)S(1)} %copy-done.5, bf16[4,1024,2048]{2,1,0:T(8,128)(2,1)S(1)} %copy-done, f32[8,128]{1,0:T(8,128)S(1)} %copy-done.1, f32[1,128]{1,0:T(1,128)S(1)} %bitcast.7, ...), custom_call_target="tpu_custom_call", output_to_operand_aliasing={{}: (10, {})} | custom-call | flops 536870912 | bytes 1048576 | tf_op jit(solution)/shard_map/pallas_call | solution.py:199
  40.1 1.9 %collective-permute-start.16 = (bf16[1024,128]{1,0:T(8,128)(2,1)S(1)}, bf16[1024,128]{1,0:T(8,128)(2,1)S(1)}, u32[]{:S(2)}, u32[]{:S(2)}) collective-permute-start(bf16[1024,128]{1,0:T(8,128)(2,1)S(1)} %get-tuple-element.6.refs_0_), channel_id=1, source_target_pairs={{0,8},{2,6},{8,16},{10,2},{16,24},{18,10},{24,28},{26,18},{28,20},... | collective-permute-start | bytes 786440 | tf_op jit(solution)/shard_map/ppermute | solution.py:239
  43.5 3.0 %collective-permute-done.16.refs_0_ = bf16[1024,128]{1,0:T(8,128)(2,1)S(1)} collective-permute-done((bf16[1024,128]{1,0:T(8,128)(2,1)S(1)}, bf16[1024,128]{1,0:T(8,128)(2,1)S(1)}, u32[]{:S(2)}, u32[]{:S(2)}) %collective-permute-start.16) | collective-permute-done | bytes 262176 | tf_op jit(solution)/shard_map/ppermute | solution.py:239
  46.5 1.9 %collective-permute-start.17 = (bf16[1024,128]{1,0:T(8,128)(2,1)S(1)}, bf16[1024,128]{1,0:T(8,128)(2,1)S(1)}, u32[]{:S(2)}, u32[]{:S(2)}) collective-permute-start(bf16[1024,128]{1,0:T(8,128)(2,1)S(1)} %collective-permute-done.16.refs_0_), channel_id=1, source_target_pairs={{0,8},{2,6},{8,16},{10,2},{16,24},{18,10},{24,28},{26,18},{28,20},... | collective-permute-start | bytes 786440 | tf_op jit(solution)/shard_map/ppermute | solution.py:245
  49.3 1.9 %collective-permute-start.23 = (bf16[1024,128]{1,0:T(8,128)(2,1)S(1)}, bf16[1024,128]{1,0:T(8,128)(2,1)S(1)}, u32[]{:S(2)}, u32[]{:S(2)}) collective-permute-start(bf16[1024,128]{1,0:T(8,128)(2,1)S(1)} %collective-permute-done.22.refs_1_), channel_id=1, source_target_pairs={{0,8},{2,6},{8,16},{10,2},{16,24},{18,10},{24,28},{26,18},{28,20},... | collective-permute-start | bytes 786440 | tf_op jit(solution)/shard_map/ppermute | solution.py:248
  52.9 1.9 %collective-permute-start.18 = (bf16[1024,128]{1,0:T(8,128)(2,1)S(1)}, bf16[1024,128]{1,0:T(8,128)(2,1)S(1)}, u32[]{:S(2)}, u32[]{:S(2)}) collective-permute-start(bf16[1024,128]{1,0:T(8,128)(2,1)S(1)} %collective-permute-done.17.refs_0_), channel_id=1, source_target_pairs={{0,8},{2,6},{8,16},{10,2},{16,24},{18,10},{24,28},{26,18},{28,20},... | collective-permute-start | bytes 786440 | tf_op jit(solution)/shard_map/ppermute | solution.py:245
  59.3 1.9 %collective-permute-start.19 = (bf16[1024,128]{1,0:T(8,128)(2,1)S(1)}, bf16[1024,128]{1,0:T(8,128)(2,1)S(1)}, u32[]{:S(2)}, u32[]{:S(2)}) collective-permute-start(bf16[1024,128]{1,0:T(8,128)(2,1)S(1)} %collective-permute-done.18.refs_0_), channel_id=1, source_target_pairs={{0,8},{2,6},{8,16},{10,2},{16,24},{18,10},{24,28},{26,18},{28,20},... | collective-permute-start | bytes 786440 | tf_op jit(solution)/shard_map/ppermute | solution.py:245
  62.9 2.8 %collective-permute-done.19.refs_0_ = bf16[1024,128]{1,0:T(8,128)(2,1)S(1)} collective-permute-done((bf16[1024,128]{1,0:T(8,128)(2,1)S(1)}, bf16[1024,128]{1,0:T(8,128)(2,1)S(1)}, u32[]{:S(2)}, u32[]{:S(2)}) %collective-permute-start.19) | collective-permute-done | bytes 262176 | tf_op jit(solution)/shard_map/ppermute | solution.py:245
  65.7 1.8 %shard_map.111.refs_4_ = f32[1024,128]{1,0:T(8,128)S(1)} custom-call(s32[2]{0:T(128)S(1)} %pad_add_fusion.where, s32[1,4]{1,0:T(1,128)S(1)} %copy-done.4, s32[1,4]{1,0:T(1,128)S(1)} %copy-done.5, bf16[4,1024,2048]{2,1,0:T(8,128)(2,1)S(1)} %copy-done, f32[8,128]{1,0:T(8,128)S(1)} %copy-done.1, f32[1,128]{1,0:T(1,128)S(1)} %bitcast.10, ...), custom_call_target="tpu_custom_call" | custom-call | flops 268435456 | bytes 1048576 | tf_op jit(solution)/shard_map/pallas_call | solution.py:199
  67.5 2.0 %shard_map.112.refs_4_ = f32[1024,128]{1,0:T(8,128)S(1)} custom-call(s32[2]{0:T(128)S(1)} %pad_add_fusion.where, s32[1,4]{1,0:T(1,128)S(1)} %copy-done.4, s32[1,4]{1,0:T(1,128)S(1)} %copy-done.5, bf16[4,1024,2048]{2,1,0:T(8,128)(2,1)S(1)} %copy-done, f32[8,128]{1,0:T(8,128)S(1)} %copy-done.1, ...), custom_call_target="tpu_custom_call", output_to_operand_aliasing={{}: (10, {})} | custom-call | flops 536870912 | bytes 1048576 | tf_op jit(solution)/shard_map/pallas_call | solution.py:199
  70.2 1.7 %shard_map.114.refs_4_ = f32[1024,128]{1,0:T(8,128)S(1)} custom-call(s32[2]{0:T(128)S(1)} %pad_add_fusion.where, s32[1,4]{1,0:T(1,128)S(1)} %copy-done.4, s32[1,4]{1,0:T(1,128)S(1)} %copy-done.5, bf16[4,1024,2048]{2,1,0:T(8,128)(2,1)S(1)} %copy-done, f32[8,128]{1,0:T(8,128)S(1)} %copy-done.1, ...), custom_call_target="tpu_custom_call", output_to_operand_aliasing={{}: (11, {})} | custom-call | bytes 1048576 | tf_op jit(solution)/shard_map/pallas_call | solution.py:199
  71.9 3.1 %shard_map.115.refs_1_ = f32[1024,128]{1,0:T(8,128)S(1)} custom-call(s32[2]{0:T(128)S(1)} %pad_add_fusion.where, s32[1,4]{1,0:T(1,128)S(1)} %copy-done.4, s32[1,4]{1,0:T(1,128)S(1)} %copy-done.5, bf16[4,1024,2048]{2,1,0:T(8,128)(2,1)S(1)} %copy-done, f32[8,128]{1,0:T(8,128)S(1)} %copy-done.1, ...), custom_call_target="tpu_custom_call", output_to_operand_aliasing={{}: (10, {})} | custom-call | flops 536870912 | bytes 1048576 | tf_op jit(solution)/shard_map/pallas_call | solution.py:199
  76.9 1.9 %collective-permute-start.32 = (bf16[1024,128]{1,0:T(8,128)(2,1)S(1)}, bf16[1024,128]{1,0:T(8,128)(2,1)S(1)}, u32[]{:S(2)}, u32[]{:S(2)}) collective-permute-start(bf16[1024,128]{1,0:T(8,128)(2,1)S(1)} %get-tuple-element.8.refs_0_), channel_id=1, source_target_pairs={{0,8},{2,6},{8,16},{10,2},{16,24},{18,10},{24,28},{26,18},{28,20},... | collective-permute-start | bytes 786440 | tf_op jit(solution)/shard_map/ppermute | solution.py:239
  80.2 3.1 %collective-permute-done.32.refs_0_ = bf16[1024,128]{1,0:T(8,128)(2,1)S(1)} collective-permute-done((bf16[1024,128]{1,0:T(8,128)(2,1)S(1)}, bf16[1024,128]{1,0:T(8,128)(2,1)S(1)}, u32[]{:S(2)}, u32[]{:S(2)}) %collective-permute-start.32) | collective-permute-done | bytes 262176 | tf_op jit(solution)/shard_map/ppermute | solution.py:239
  83.3 1.9 %collective-permute-start.33 = (bf16[1024,128]{1,0:T(8,128)(2,1)S(1)}, bf16[1024,128]{1,0:T(8,128)(2,1)S(1)}, u32[]{:S(2)}, u32[]{:S(2)}) collective-permute-start(bf16[1024,128]{1,0:T(8,128)(2,1)S(1)} %collective-permute-done.32.refs_0_), channel_id=1, source_target_pairs={{0,8},{2,6},{8,16},{10,2},{16,24},{18,10},{24,28},{26,18},{28,20},... | collective-permute-start | bytes 786440 | tf_op jit(solution)/shard_map/ppermute | solution.py:245
  86.1 1.9 %collective-permute-start.39 = (bf16[1024,128]{1,0:T(8,128)(2,1)S(1)}, bf16[1024,128]{1,0:T(8,128)(2,1)S(1)}, u32[]{:S(2)}, u32[]{:S(2)}) collective-permute-start(bf16[1024,128]{1,0:T(8,128)(2,1)S(1)} %collective-permute-done.38.refs_1_), channel_id=1, source_target_pairs={{0,8},{2,6},{8,16},{10,2},{16,24},{18,10},{24,28},{26,18},{28,20},... | collective-permute-start | bytes 786440 | tf_op jit(solution)/shard_map/ppermute | solution.py:248
  89.7 1.9 %collective-permute-start.34 = (bf16[1024,128]{1,0:T(8,128)(2,1)S(1)}, bf16[1024,128]{1,0:T(8,128)(2,1)S(1)}, u32[]{:S(2)}, u32[]{:S(2)}) collective-permute-start(bf16[1024,128]{1,0:T(8,128)(2,1)S(1)} %collective-permute-done.33.refs_0_), channel_id=1, source_target_pairs={{0,8},{2,6},{8,16},{10,2},{16,24},{18,10},{24,28},{26,18},{28,20},... | collective-permute-start | bytes 786440 | tf_op jit(solution)/shard_map/ppermute | solution.py:245
  96.0 1.9 %collective-permute-start.35 = (bf16[1024,128]{1,0:T(8,128)(2,1)S(1)}, bf16[1024,128]{1,0:T(8,128)(2,1)S(1)}, u32[]{:S(2)}, u32[]{:S(2)}) collective-permute-start(bf16[1024,128]{1,0:T(8,128)(2,1)S(1)} %collective-permute-done.34.refs_0_), channel_id=1, source_target_pairs={{0,8},{2,6},{8,16},{10,2},{16,24},{18,10},{24,28},{26,18},{28,20},... | collective-permute-start | bytes 786440 | tf_op jit(solution)/shard_map/ppermute | solution.py:245
  99.7 2.8 %collective-permute-done.35.refs_0_ = bf16[1024,128]{1,0:T(8,128)(2,1)S(1)} collective-permute-done((bf16[1024,128]{1,0:T(8,128)(2,1)S(1)}, bf16[1024,128]{1,0:T(8,128)(2,1)S(1)}, u32[]{:S(2)}, u32[]{:S(2)}) %collective-permute-start.35) | collective-permute-done | bytes 262176 | tf_op jit(solution)/shard_map/ppermute | solution.py:245
  103.3 1.8 %shard_map.118.refs_4_ = f32[1024,128]{1,0:T(8,128)S(1)} custom-call(s32[2]{0:T(128)S(1)} %pad_add_fusion.where, s32[1,4]{1,0:T(1,128)S(1)} %copy-done.4, s32[1,4]{1,0:T(1,128)S(1)} %copy-done.5, bf16[4,1024,2048]{2,1,0:T(8,128)(2,1)S(1)} %copy-done, f32[8,128]{1,0:T(8,128)S(1)} %copy-done.1, f32[1,128]{1,0:T(1,128)S(1)} %bitcast.17, ...), custom_call_target="tpu_custom_call" | custom-call | flops 268435456 | bytes 1048576 | tf_op jit(solution)/shard_map/pallas_call | solution.py:199
  105.1 1.8 %shard_map.119.refs_4_ = f32[1024,128]{1,0:T(8,128)S(1)} custom-call(s32[2]{0:T(128)S(1)} %pad_add_fusion.where, s32[1,4]{1,0:T(1,128)S(1)} %copy-done.4, s32[1,4]{1,0:T(1,128)S(1)} %copy-done.5, bf16[4,1024,2048]{2,1,0:T(8,128)(2,1)S(1)} %copy-done, f32[8,128]{1,0:T(8,128)S(1)} %copy-done.1, ...), custom_call_target="tpu_custom_call", output_to_operand_aliasing={{}: (10, {})} | custom-call | flops 536870912 | bytes 1048576 | tf_op jit(solution)/shard_map/pallas_call | solution.py:199
  109.0 3.1 %shard_map.122.refs_1_ = f32[1024,128]{1,0:T(8,128)S(1)} custom-call(s32[2]{0:T(128)S(1)} %pad_add_fusion.where, s32[1,4]{1,0:T(1,128)S(1)} %copy-done.4, s32[1,4]{1,0:T(1,128)S(1)} %copy-done.5, bf16[4,1024,2048]{2,1,0:T(8,128)(2,1)S(1)} %copy-done, f32[8,128]{1,0:T(8,128)S(1)} %copy-done.1, ...), custom_call_target="tpu_custom_call", output_to_operand_aliasing={{}: (10, {})} | custom-call | flops 536870912 | bytes 1048576 | tf_op jit(solution)/shard_map/pallas_call | solution.py:199
  (105 shorter events, 42.0 us)
Async XLA Ops:
  2.5 6.9 %collective-permute-start = (bf16[1024,128]{1,0:T(8,128)(2,1)S(1)}, bf16[1024,128]{1,0:T(8,128)(2,1)S(1)}, u32[]{:S(2)}, u32[]{:S(2)}) collective-permute-start(bf16[1024,128]{1,0:T(8,128)(2,1)S(1)} %prepare.1.refs_0_), channel_id=1, source_target_pairs={{0,8},{2,6},{8,16},{10,2},{16,24},{18,10},{24,28},{26,18},{28,20},... | collective-permute-start | bytes 786440 | tf_op jit(solution)/shard_map/ppermute | solution.py:239
  5.2 7.1 %collective-permute-start.6 = (bf16[1024,128]{1,0:T(8,128)(2,1)S(1)}, bf16[1024,128]{1,0:T(8,128)(2,1)S(1)}, u32[]{:S(2)}, u32[]{:S(2)}) collective-permute-start(bf16[1024,128]{1,0:T(8,128)(2,1)S(1)} %collective-permute-done.5.refs_1_), channel_id=1, source_target_pairs={{0,8},{2,6},{8,16},{10,2},{16,24},{18,10},{24,28},{26,18},{28,20},... | collective-permute-start | bytes 786440 | tf_op jit(solution)/shard_map/ppermute | solution.py:242
  11.5 7.9 %collective-permute-start.14 = (bf16[1024,128]{1,0:T(8,128)(2,1)S(1)}, bf16[1024,128]{1,0:T(8,128)(2,1)S(1)}, u32[]{:S(2)}, u32[]{:S(2)}) collective-permute-start(bf16[1024,128]{1,0:T(8,128)(2,1)S(1)} %collective-permute-done.refs_0_), channel_id=1, source_target_pairs={{0,2},{2,0},{4,6},{6,4},{8,10},{10,8},{12,14},{14,12},{16,18},{18,... | collective-permute-start | bytes 786440 | tf_op jit(solution)/shard_map/ppermute | solution.py:246
  12.3 7.4 %collective-permute-start.7 = (bf16[1024,128]{1,0:T(8,128)(2,1)S(1)}, bf16[1024,128]{1,0:T(8,128)(2,1)S(1)}, u32[]{:S(2)}, u32[]{:S(2)}) collective-permute-start(bf16[1024,128]{1,0:T(8,128)(2,1)S(1)} %collective-permute-done.6.refs_1_), channel_id=1, source_target_pairs={{0,8},{2,6},{8,16},{10,2},{16,24},{18,10},{24,28},{26,18},{28,20},... | collective-permute-start | bytes 786440 | tf_op jit(solution)/shard_map/ppermute | solution.py:248
  17.9 6.4 %collective-permute-start.15 = (bf16[1024,128]{1,0:T(8,128)(2,1)S(1)}, bf16[1024,128]{1,0:T(8,128)(2,1)S(1)}, u32[]{:S(2)}, u32[]{:S(2)}) collective-permute-start(bf16[1024,128]{1,0:T(8,128)(2,1)S(1)} %collective-permute-done.6.refs_1_), channel_id=1, source_target_pairs={{0,2},{2,0},{4,6},{6,4},{8,10},{10,8},{12,14},{14,12},{16,18},{18,... | collective-permute-start | bytes 786440 | tf_op jit(solution)/shard_map/ppermute | solution.py:249
  17.9 15.3 %collective-permute-start.11 = (f32[1024,128]{1,0:T(8,128)}, f32[1024,128]{1,0:T(8,128)S(1)}, u32[]{:S(2)}, u32[]{:S(2)}) collective-permute-start(f32[1024,128]{1,0:T(8,128)} %refs_1_.3), channel_id=1, source_target_pairs={{0,1},{1,0},{2,3},{3,2},{4,5},{5,4},{6,7},{7,6},{8,9},{9,8},{10,11... | collective-permute-start | bytes 1572872 | tf_op jit(solution)/shard_map/ppermute | solution.py:241
  22.2 6.6 %collective-permute-start.3 = (bf16[1024,128]{1,0:T(8,128)(2,1)S(1)}, bf16[1024,128]{1,0:T(8,128)(2,1)S(1)}, u32[]{:S(2)}, u32[]{:S(2)}) collective-permute-start(bf16[1024,128]{1,0:T(8,128)(2,1)S(1)} %collective-permute-done.2.refs_0_), channel_id=1, source_target_pairs={{0,8},{2,6},{8,16},{10,2},{16,24},{18,10},{24,28},{26,18},{28,20},... | collective-permute-start | bytes 786440 | tf_op jit(solution)/shard_map/ppermute | solution.py:245
  24.3 8.3 %collective-permute-start.13 = (bf16[1024,128]{1,0:T(8,128)(2,1)S(1)}, bf16[1024,128]{1,0:T(8,128)(2,1)S(1)}, u32[]{:S(2)}, u32[]{:S(2)}) collective-permute-start(bf16[1024,128]{1,0:T(8,128)(2,1)S(1)} %collective-permute-done.7.refs_1_), channel_id=1, source_target_pairs={{0,2},{2,0},{4,6},{6,4},{8,10},{10,8},{12,14},{14,12},{16,18},{18,... | collective-permute-start | bytes 786440 | tf_op jit(solution)/shard_map/ppermute | solution.py:249
  24.3 10.9 %collective-permute-start.9 = (bf16[1024,128]{1,0:T(8,128)(2,1)S(1)}, bf16[1024,128]{1,0:T(8,128)(2,1)S(1)}, u32[]{:S(2)}, u32[]{:S(2)}) collective-permute-start(bf16[1024,128]{1,0:T(8,128)(2,1)S(1)} %collective-permute-done.2.refs_0_), channel_id=1, source_target_pairs={{0,2},{2,0},{4,6},{6,4},{8,10},{10,8},{12,14},{14,12},{16,18},{18,... | collective-permute-start | bytes 786440 | tf_op jit(solution)/shard_map/ppermute | solution.py:246
  26.0 9.2 %collective-permute-start.10 = (bf16[1024,128]{1,0:T(8,128)(2,1)S(1)}, bf16[1024,128]{1,0:T(8,128)(2,1)S(1)}, u32[]{:S(2)}, u32[]{:S(2)}) collective-permute-start(bf16[1024,128]{1,0:T(8,128)(2,1)S(1)} %collective-permute-done.8.refs_1_), channel_id=1, source_target_pairs={{0,2},{2,0},{4,6},{6,4},{8,10},{10,8},{12,14},{14,12},{16,18},{18,... | collective-permute-start | bytes 786440 | tf_op jit(solution)/shard_map/ppermute | solution.py:249
  28.8 10.0 %collective-permute-start.4 = (bf16[1024,128]{1,0:T(8,128)(2,1)S(1)}, bf16[1024,128]{1,0:T(8,128)(2,1)S(1)}, u32[]{:S(2)}, u32[]{:S(2)}) collective-permute-start(bf16[1024,128]{1,0:T(8,128)(2,1)S(1)} %collective-permute-done.3.refs_0_), channel_id=1, source_target_pairs={{0,2},{2,0},{4,6},{6,4},{8,10},{10,8},{12,14},{14,12},{16,18},{18,... | collective-permute-start | bytes 786440 | tf_op jit(solution)/shard_map/ppermute | solution.py:255
  42.1 7.3 %collective-permute-start.22 = (bf16[1024,128]{1,0:T(8,128)(2,1)S(1)}, bf16[1024,128]{1,0:T(8,128)(2,1)S(1)}, u32[]{:S(2)}, u32[]{:S(2)}) collective-permute-start(bf16[1024,128]{1,0:T(8,128)(2,1)S(1)} %collective-permute-done.21.refs_1_), channel_id=1, source_target_pairs={{0,8},{2,6},{8,16},{10,2},{16,24},{18,10},{24,28},{26,18},{28,20},... | collective-permute-start | bytes 786440 | tf_op jit(solution)/shard_map/ppermute | solution.py:242
  48.4 7.9 %collective-permute-start.30 = (bf16[1024,128]{1,0:T(8,128)(2,1)S(1)}, bf16[1024,128]{1,0:T(8,128)(2,1)S(1)}, u32[]{:S(2)}, u32[]{:S(2)}) collective-permute-start(bf16[1024,128]{1,0:T(8,128)(2,1)S(1)} %collective-permute-done.16.refs_0_), channel_id=1, source_target_pairs={{0,2},{2,0},{4,6},{6,4},{8,10},{10,8},{12,14},{14,12},{16,18},{18,... | collective-permute-start | bytes 786440 | tf_op jit(solution)/shard_map/ppermute | solution.py:246
  49.3 7.2 %collective-permute-start.23 = (bf16[1024,128]{1,0:T(8,128)(2,1)S(1)}, bf16[1024,128]{1,0:T(8,128)(2,1)S(1)}, u32[]{:S(2)}, u32[]{:S(2)}) collective-permute-start(bf16[1024,128]{1,0:T(8,128)(2,1)S(1)} %collective-permute-done.22.refs_1_), channel_id=1, source_target_pairs={{0,8},{2,6},{8,16},{10,2},{16,24},{18,10},{24,28},{26,18},{28,20},... | collective-permute-start | bytes 786440 | tf_op jit(solution)/shard_map/ppermute | solution.py:248
  54.8 6.4 %collective-permute-start.31 = (bf16[1024,128]{1,0:T(8,128)(2,1)S(1)}, bf16[1024,128]{1,0:T(8,128)(2,1)S(1)}, u32[]{:S(2)}, u32[]{:S(2)}) collective-permute-start(bf16[1024,128]{1,0:T(8,128)(2,1)S(1)} %collective-permute-done.22.refs_1_), channel_id=1, source_target_pairs={{0,2},{2,0},{4,6},{6,4},{8,10},{10,8},{12,14},{14,12},{16,18},{18,... | collective-permute-start | bytes 786440 | tf_op jit(solution)/shard_map/ppermute | solution.py:249
  54.8 15.4 %collective-permute-start.27 = (f32[1024,128]{1,0:T(8,128)S(1)}, f32[1024,128]{1,0:T(8,128)S(1)}, u32[]{:S(2)}, u32[]{:S(2)}) collective-permute-start(f32[1024,128]{1,0:T(8,128)S(1)} %get-tuple-element.7.refs_0_.refs_1_), channel_id=1, source_target_pairs={{0,1},{1,0},{2,3},{3,2},{4,5},{5,4},{6,7},{7,6},{8,9},{9,8},{10,11... | collective-permute-start | bytes 1572872 | tf_op jit(solution)/shard_map/ppermute | solution.py:241
  56.5 6.4 %collective-permute-start.24 = (bf16[1024,128]{1,0:T(8,128)(2,1)S(1)}, bf16[1024,128]{1,0:T(8,128)(2,1)S(1)}, u32[]{:S(2)}, u32[]{:S(2)}) collective-permute-start(bf16[1024,128]{1,0:T(8,128)(2,1)S(1)} %collective-permute-done.23.refs_1_), channel_id=1, source_target_pairs={{0,8},{2,6},{8,16},{10,2},{16,24},{18,10},{24,28},{26,18},{28,20},... | collective-permute-start | bytes 786440 | tf_op jit(solution)/shard_map/ppermute | solution.py:248
  59.3 6.4 %collective-permute-start.19 = (bf16[1024,128]{1,0:T(8,128)(2,1)S(1)}, bf16[1024,128]{1,0:T(8,128)(2,1)S(1)}, u32[]{:S(2)}, u32[]{:S(2)}) collective-permute-start(bf16[1024,128]{1,0:T(8,128)(2,1)S(1)} %collective-permute-done.18.refs_0_), channel_id=1, source_target_pairs={{0,8},{2,6},{8,16},{10,2},{16,24},{18,10},{24,28},{26,18},{28,20},... | collective-permute-start | bytes 786440 | tf_op jit(solution)/shard_map/ppermute | solution.py:245
  61.2 8.4 %collective-permute-start.29 = (bf16[1024,128]{1,0:T(8,128)(2,1)S(1)}, bf16[1024,128]{1,0:T(8,128)(2,1)S(1)}, u32[]{:S(2)}, u32[]{:S(2)}) collective-permute-start(bf16[1024,128]{1,0:T(8,128)(2,1)S(1)} %collective-permute-done.23.refs_1_), channel_id=1, source_target_pairs={{0,2},{2,0},{4,6},{6,4},{8,10},{10,8},{12,14},{14,12},{16,18},{18,... | collective-permute-start | bytes 786440 | tf_op jit(solution)/shard_map/ppermute | solution.py:249
  61.2 10.7 %collective-permute-start.25 = (bf16[1024,128]{1,0:T(8,128)(2,1)S(1)}, bf16[1024,128]{1,0:T(8,128)(2,1)S(1)}, u32[]{:S(2)}, u32[]{:S(2)}) collective-permute-start(bf16[1024,128]{1,0:T(8,128)(2,1)S(1)} %collective-permute-done.18.refs_0_), channel_id=1, source_target_pairs={{0,2},{2,0},{4,6},{6,4},{8,10},{10,8},{12,14},{14,12},{16,18},{18,... | collective-permute-start | bytes 786440 | tf_op jit(solution)/shard_map/ppermute | solution.py:246
  62.9 9.0 %collective-permute-start.26 = (bf16[1024,128]{1,0:T(8,128)(2,1)S(1)}, bf16[1024,128]{1,0:T(8,128)(2,1)S(1)}, u32[]{:S(2)}, u32[]{:S(2)}) collective-permute-start(bf16[1024,128]{1,0:T(8,128)(2,1)S(1)} %collective-permute-done.24.refs_1_), channel_id=1, source_target_pairs={{0,2},{2,0},{4,6},{6,4},{8,10},{10,8},{12,14},{14,12},{16,18},{18,... | collective-permute-start | bytes 786440 | tf_op jit(solution)/shard_map/ppermute | solution.py:249
  65.7 9.9 %collective-permute-start.20 = (bf16[1024,128]{1,0:T(8,128)(2,1)S(1)}, bf16[1024,128]{1,0:T(8,128)(2,1)S(1)}, u32[]{:S(2)}, u32[]{:S(2)}) collective-permute-start(bf16[1024,128]{1,0:T(8,128)(2,1)S(1)} %collective-permute-done.19.refs_0_), channel_id=1, source_target_pairs={{0,2},{2,0},{4,6},{6,4},{8,10},{10,8},{12,14},{14,12},{16,18},{18,... | collective-permute-start | bytes 786440 | tf_op jit(solution)/shard_map/ppermute | solution.py:255
  78.8 7.3 %collective-permute-start.38 = (bf16[1024,128]{1,0:T(8,128)(2,1)S(1)}, bf16[1024,128]{1,0:T(8,128)(2,1)S(1)}, u32[]{:S(2)}, u32[]{:S(2)}) collective-permute-start(bf16[1024,128]{1,0:T(8,128)(2,1)S(1)} %collective-permute-done.37.refs_1_), channel_id=1, source_target_pairs={{0,8},{2,6},{8,16},{10,2},{16,24},{18,10},{24,28},{26,18},{28,20},... | collective-permute-start | bytes 786440 | tf_op jit(solution)/shard_map/ppermute | solution.py:242
  85.2 7.9 %collective-permute-start.46 = (bf16[1024,128]{1,0:T(8,128)(2,1)S(1)}, bf16[1024,128]{1,0:T(8,128)(2,1)S(1)}, u32[]{:S(2)}, u32[]{:S(2)}) collective-permute-start(bf16[1024,128]{1,0:T(8,128)(2,1)S(1)} %collective-permute-done.32.refs_0_), channel_id=1, source_target_pairs={{0,2},{2,0},{4,6},{6,4},{8,10},{10,8},{12,14},{14,12},{16,18},{18,... | collective-permute-start | bytes 786440 | tf_op jit(solution)/shard_map/ppermute | solution.py:246
  86.1 7.2 %collective-permute-start.39 = (bf16[1024,128]{1,0:T(8,128)(2,1)S(1)}, bf16[1024,128]{1,0:T(8,128)(2,1)S(1)}, u32[]{:S(2)}, u32[]{:S(2)}) collective-permute-start(bf16[1024,128]{1,0:T(8,128)(2,1)S(1)} %collective-permute-done.38.refs_1_), channel_id=1, source_target_pairs={{0,8},{2,6},{8,16},{10,2},{16,24},{18,10},{24,28},{26,18},{28,20},... | collective-permute-start | bytes 786440 | tf_op jit(solution)/shard_map/ppermute | solution.py:248
  91.6 6.4 %collective-permute-start.47 = (bf16[1024,128]{1,0:T(8,128)(2,1)S(1)}, bf16[1024,128]{1,0:T(8,128)(2,1)S(1)}, u32[]{:S(2)}, u32[]{:S(2)}) collective-permute-start(bf16[1024,128]{1,0:T(8,128)(2,1)S(1)} %collective-permute-done.38.refs_1_), channel_id=1, source_target_pairs={{0,2},{2,0},{4,6},{6,4},{8,10},{10,8},{12,14},{14,12},{16,18},{18,... | collective-permute-start | bytes 786440 | tf_op jit(solution)/shard_map/ppermute | solution.py:249
  91.6 16.2 %collective-permute-start.43 = (f32[1024,128]{1,0:T(8,128)S(1)}, f32[1024,128]{1,0:T(8,128)S(1)}, u32[]{:S(2)}, u32[]{:S(2)}) collective-permute-start(f32[1024,128]{1,0:T(8,128)S(1)} %get-tuple-element.11.refs_0_), channel_id=1, source_target_pairs={{0,1},{1,0},{2,3},{3,2},{4,5},{5,4},{6,7},{7,6},{8,9},{9,8},{10,11... | collective-permute-start | bytes 1572872 | tf_op jit(solution)/shard_map/ppermute | solution.py:241
  96.0 6.5 %collective-permute-start.35 = (bf16[1024,128]{1,0:T(8,128)(2,1)S(1)}, bf16[1024,128]{1,0:T(8,128)(2,1)S(1)}, u32[]{:S(2)}, u32[]{:S(2)}) collective-permute-start(bf16[1024,128]{1,0:T(8,128)(2,1)S(1)} %collective-permute-done.34.refs_0_), channel_id=1, source_target_pairs={{0,8},{2,6},{8,16},{10,2},{16,24},{18,10},{24,28},{26,18},{28,20},... | collective-permute-start | bytes 786440 | tf_op jit(solution)/shard_map/ppermute | solution.py:245
  98.0 9.0 %collective-permute-start.45 = (bf16[1024,128]{1,0:T(8,128)(2,1)S(1)}, bf16[1024,128]{1,0:T(8,128)(2,1)S(1)}, u32[]{:S(2)}, u32[]{:S(2)}) collective-permute-start(bf16[1024,128]{1,0:T(8,128)(2,1)S(1)} %collective-permute-done.39.refs_1_), channel_id=1, source_target_pairs={{0,2},{2,0},{4,6},{6,4},{8,10},{10,8},{12,14},{14,12},{16,18},{18,... | collective-permute-start | bytes 786440 | tf_op jit(solution)/shard_map/ppermute | solution.py:249
  98.0 11.1 %collective-permute-start.41 = (bf16[1024,128]{1,0:T(8,128)(2,1)S(1)}, bf16[1024,128]{1,0:T(8,128)(2,1)S(1)}, u32[]{:S(2)}, u32[]{:S(2)}) collective-permute-start(bf16[1024,128]{1,0:T(8,128)(2,1)S(1)} %collective-permute-done.34.refs_0_), channel_id=1, source_target_pairs={{0,2},{2,0},{4,6},{6,4},{8,10},{10,8},{12,14},{14,12},{16,18},{18,... | collective-permute-start | bytes 786440 | tf_op jit(solution)/shard_map/ppermute | solution.py:246
  99.7 9.3 %collective-permute-start.42 = (bf16[1024,128]{1,0:T(8,128)(2,1)S(1)}, bf16[1024,128]{1,0:T(8,128)(2,1)S(1)}, u32[]{:S(2)}, u32[]{:S(2)}) collective-permute-start(bf16[1024,128]{1,0:T(8,128)(2,1)S(1)} %collective-permute-done.40.refs_1_), channel_id=1, source_target_pairs={{0,2},{2,0},{4,6},{6,4},{8,10},{10,8},{12,14},{14,12},{16,18},{18,... | collective-permute-start | bytes 786440 | tf_op jit(solution)/shard_map/ppermute | solution.py:249
  102.5 10.2 %collective-permute-start.36 = (bf16[1024,128]{1,0:T(8,128)(2,1)S(1)}, bf16[1024,128]{1,0:T(8,128)(2,1)S(1)}, u32[]{:S(2)}, u32[]{:S(2)}) collective-permute-start(bf16[1024,128]{1,0:T(8,128)(2,1)S(1)} %collective-permute-done.35.refs_0_), channel_id=1, source_target_pairs={{0,2},{2,0},{4,6},{6,4},{8,10},{10,8},{12,14},{14,12},{16,18},{18,... | collective-permute-start | bytes 786440 | tf_op jit(solution)/shard_map/ppermute | solution.py:255
  (24 other events, 235.1 us)
where the time goes:
time: 114 us
  starting transfers between devices  47.3 us (41%)
  Pallas kernels  32.8 us (29%)
  waiting for transfers between devices  31.9 us (28%)
    pallas_call x21, Pallas kernels, run(): pl.pallas_call(kernel, out_shape=outs, in_specs=specs, out_specs=[VSPEC]...  31.6 us
    ppermute x9, starting transfers between devices, local(): next_p = lax.ppermute(p, 'chan', ring)  17.7 us
    ppermute x9, waiting for transfers between devices, local(): next_p = lax.ppermute(p, 'chan', ring)  16.8 us
    ppermute x6, starting transfers between devices, local(): next_q = lax.ppermute(q, 'chan', ring)  10.3 us
    ppermute x3, waiting for transfers between devices, local(): p = lax.ppermute(rounded, 'chan', ring)  8.82 us
    ppermute x3, starting transfers between devices, local(): p = lax.ppermute(rounded, 'chan', ring)  6.43 us
    ppermute x3, starting transfers between devices, local(): sides = [lax.ppermute(current, 'dist', perm) for perm in shifts]  4.49 us
    ppermute x3, starting transfers between devices, local(): q = lax.ppermute(partner, 'chan', ring)  4.4 us
  transfers between devices with their start and end apart: 48, of which 18 were waited for; matrix products, arithmetic and copies ran while one was open for 1% of the time, Pallas kernels for 25%

commit v1 on v0

--- a/solution.py
+++ b/solution.py
@@ -67,61 +67,113 @@
     return pltpu.with_memory_space_constraint(x, pltpu.VMEM)
 
 
+def smem(x):
+    return pltpu.with_memory_space_constraint(x, pltpu.SMEM)
+
+
 VSPEC = pl.BlockSpec(memory_space=pltpu.VMEM)
 SSPEC = pl.BlockSpec(memory_space=pltpu.SMEM)
 VMEM_BYTES = 12 << 20
-OWN, RING, SWAP = 0, -1, 1
-
-
-def prepare(q_now, where):
-    def kernel(where, x, out):
-        out[...] = x[...].astype(jnp.bfloat16)
+FIELDS = 3
+
+
+def slots(chips):
+    far = chips // 2
+    near = [(side, r) for r in range(1, far) for side in (-1, 1)]
+    return [(0, 0)] + near + [(-1, far)]
+
+
+def prepare(q_now):
+    def kernel(x, out, rounded):
+        value = x[...]
+        out[...] = value
+        rounded[...] = value.astype(jnp.bfloat16)
 
     return pl.pallas_call(
         kernel,
-        out_shape=pltpu.VMEM(q_now.shape, jnp.bfloat16),
-        in_specs=[SSPEC, VSPEC],
-        out_specs=VSPEC,
-        cost_estimate=pl.CostEstimate(flops=12 * 10**9, transcendentals=0, bytes_accessed=q_now.size * 6),
+        out_shape=[pltpu.VMEM(q_now.shape, q_now.dtype), pltpu.VMEM(q_now.shape, jnp.bfloat16)],
+        in_specs=[VSPEC],
+        out_specs=[VSPEC, VSPEC],
+        cost_estimate=pl.CostEstimate(flops=40 * 10**9, transcendentals=0, bytes_accessed=q_now.size * 6),
         compiler_params=pltpu.CompilerParams(vmem_limit_bytes=VMEM_BYTES),
         name="prepare",
-    )(where, q_now)
+    )(q_now)
+
+
+def scalars(col_block, lam_index, chips, rows, cols):
+    chips_per_block = cols // (CORES * rows)
+    table = slots(chips)
+
+    def kernel(col, lam, info):
+        me = lax.axis_index("chan").astype(jnp.int32)
+        core = lax.rem(me, CORES)
+        own = lax.div(me, CORES)
+        place = place_of(own, chips)
+        way = 1 - 2 * core
+        info[0] = core
+        info[1] = lax.axis_index("dist").astype(jnp.int32)
+        for slot, (side, distance) in enumerate(table):
+            chip = own if side == 0 else chip_at(place + side * way * distance, chips)
+            block = lax.div(chip, chips_per_block)
+            which = jnp.int32(-1)
+            level = jnp.int32(0)
+            for j in range(col_block.shape[1]):
+                hit = col[0, j] == block
+                which = jnp.where(hit, j, which)
+                level = jnp.where(hit, lam[0, j], level)
+            info[2 + FIELDS * slot] = which
+            info[3 + FIELDS * slot] = level
+            info[4 + FIELDS * slot] = lax.rem(chip, chips_per_block) * (CORES * rows)
+
+    return pl.pallas_call(
+        kernel,
+        out_shape=pltpu.SMEM((2 + FIELDS * len(table),), jnp.int32),
+        in_specs=[SSPEC] * 2,
+        out_specs=SSPEC,
+        compiler_params=pltpu.CompilerParams(vmem_limit_bytes=VMEM_BYTES),
+        name="scalars",
+    )(col_block, lam_index)
+
+
+def store(x):
+    def kernel(x, out):
+        out[...] = x[...]
+
+    return pl.pallas_call(
+        kernel,
+        out_shape=jax.ShapeDtypeStruct(x.shape, x.dtype),
+        in_specs=[VSPEC],
+        out_specs=VSPEC,
+        compiler_params=pltpu.CompilerParams(vmem_limit_bytes=VMEM_BYTES),
+    )(vmem(x))
 
 
 class Stages:
-    def __init__(self, chips, shape, panels, nbrs, common):
-        self.chips = chips
+    def __init__(self, chips, shape, nbrs, common):
+        self.table = slots(chips)
         self.rows, self.points = shape
-        self.panels_n, _, self.cols = panels.shape
         self.nbrs = nbrs
         self.common = common
 
     def run(self, parts, acc=None, base=(), out="acc"):
-        rows, points, cols, chips = self.rows, self.points, self.cols, self.chips
-        chips_per_block = cols // (CORES * rows)
+        rows, points = self.rows, self.points
         first = acc is None
         counts = [len(shards) for _, _, shards in parts]
 
-        def kernel(where, col, lam, panels, radial, damp, *refs):
+        def kernel(info, panels, radial, damp, *refs):
             refs = list(refs)
             shards = [[refs.pop(0) for _ in range(n)] for n in counts]
             terms = [refs.pop(0) for _ in base]
             old = None if first else refs.pop(0)
             new = refs.pop(0)
             rounded = refs.pop(0) if out == "both" else None
-            me = where[0]
-            core = lax.rem(me, CORES)
-            place = place_of(lax.div(me, CORES), chips)
-            way = 1 - 2 * core
+            core = info[0]
             scale = damp[...]
 
             def write(value):
                 new[...] = value
                 if rounded is not None:
                     rounded[...] = value.astype(jnp.bfloat16)
-
-            if first:
-                new[...] = jnp.zeros_like(new)
 
             if base:
                 cur, before, energy, mats = terms[:4]
@@ -130,7 +182,7 @@
                 highs = [v.astype(jnp.bfloat16) for v in values]
                 lows = [(v - h.astype(jnp.float32)).astype(jnp.bfloat16) for v, h in zip(values, highs)]
                 if self.nbrs == 1:
-                    picks = [0, jnp.where(where[1] == 0, 2, 1)]
+                    picks = [0, jnp.where(info[1] == 0, 2, 1)]
                 else:
                     picks = list(range(len(values)))
                 join = lambda xs, axis: jnp.concatenate(xs, axis=axis) if len(xs) > 1 else xs[0]
@@ -142,19 +194,13 @@
                 old = new
 
             for at, ((side, distance, described), shard_refs) in enumerate(zip(parts, shards)):
-                if side == OWN:
-                    chip = lax.div(me, CORES)
-                else:
-                    chip = chip_at(place + side * way * distance, chips)
-                block = lax.div(chip, chips_per_block)
-                start = lax.rem(chip, chips_per_block) * (CORES * rows)
-                which = jnp.int32(0)
-                found = col[0, 0] == block
-                for j in range(1, self.panels_n):
-                    hit = col[0, j] == block
-                    which = jnp.where(hit, j, which)
-                    found = found | hit
-                source = new if first or base or at else old
+                slot = self.table.index((side, distance))
+                which = info[2 + FIELDS * slot]
+                level = info[3 + FIELDS * slot]
+                start = info[4 + FIELDS * slot]
+                found = which >= 0
+                source = new if base or at else old
+                end = at == len(parts) - 1
 
                 @pl.when(found)
                 def _():
@@ -164,22 +210,23 @@
                         off = pl.multiple_of(start + of_core * rows, 128)
                         part = jnp.dot(panels[which, :, pl.ds(off, rows)], shard[...], preferred_element_type=jnp.float32)
                         total = part if total is None else total + part
-                    weight = 2.0 * scale * radial[pl.ds(lam[0, which], 1), :]
-                    value = source[...] + weight * total
-                    if at == len(parts) - 1:
+                    value = 2.0 * scale * radial[pl.ds(level, 1), :] * total
+                    if source is not None:
+                        value = source[...] + value
+                    if end:
                         write(value)
                     else:
                         new[...] = value
 
-                if out != "acc" and at == len(parts) - 1:
+                if source is None or (out != "acc" and end):
 
                     @pl.when(jnp.logical_not(found))
                     def _():
-                        write(source[...])
-
-        where, col, lam, panels, radial, damp = self.common
-        args = [where, col, lam, vmem(panels), radial, damp]
-        specs = [SSPEC] * 3 + [VSPEC] * 3
+                        write(jnp.zeros_like(new) if source is None else source[...])
+
+        info, panels, radial, damp = self.common
+        args = [smem(info), vmem(panels), vmem(radial), vmem(damp)]
+        specs = [SSPEC] + [VSPEC] * 3
         for x in [shard for _, _, shards in parts for _, shard in shards] + list(base):
             args.append(vmem(x))
             specs.append(VSPEC)
@@ -216,7 +263,6 @@
     chips = count // CORES
     far = chips // 2
     rows, points = q_now.shape
-    where = jnp.stack([lax.axis_index("chan"), lax.axis_index("dist")]).astype(jnp.int32)
     ring = ring_perm(chips)
     swap = [(i, i ^ 1) for i in range(count)]
     energy = jnp.broadcast_to(energies[:, None], (rows, points))
@@ -229,38 +275,77 @@
         shifts = [right + left]
     else:
         shifts = [right, left]
-    common = (where, col_block, lam_index, panels, radial, damping[None, :])
-    stages = Stages(chips, (rows, points), panels, len(shifts), common)
-
-    current, before = q_now, q_prev
-    rounded = prepare(q_now, where)
+    start, rounded = prepare(q_now)
+    info = scalars(col_block, lam_index, chips, rows, panels.shape[2])
+    stages = Stages(chips, (rows, points), len(shifts), (info, panels, radial, damping[None, :]))
+
+    def send(x, axis, perm):
+        return lax.ppermute(x, axis, perm)
+
+    current, before = start, q_prev
+    kept = None
     for turn in range(KCHEB):
         final = turn == KCHEB - 1
-        p = lax.ppermute(rounded, "chan", ring)
-        partner = lax.ppermute(rounded, "chan", swap)
-        sides = [lax.ppermute(current, "dist", perm) for perm in shifts]
-        q = lax.ppermute(partner, "chan", ring)
-        acc = stages.run([(OWN, 0, ((0, rounded), (1, partner)))])
-        for r in range(1, far):
-            next_p = lax.ppermute(p, "chan", ring)
-            swap_p = lax.ppermute(p, "chan", swap)
-            if r + 1 < far:
-                next_q = lax.ppermute(q, "chan", ring)
-            swap_q = lax.ppermute(q, "chan", swap)
-            parts = [(RING, r, ((0, p), (1, q))), (SWAP, r, ((1, swap_p), (0, swap_q)))]
-            if r + 1 == far:
+        have = {"rounded": rounded}
+        acc = None
+        for token in plan(far, len(shifts), final):
+            kind, r = token[0], token[1]
+            if kind == "p":
+                have[f"p{r}"] = send(have[f"p{r - 1}"] if r > 1 else rounded, "chan", ring)
+            elif kind == "q":
+                have[f"q{r}"] = send(have[f"q{r - 1}"] if r > 1 else have["sp0"], "chan", ring)
+            elif kind == "sp":
+                have[f"sp{r}"] = send(have[f"p{r}"] if r else rounded, "chan", swap)
+            elif kind == "sq":
+                have[f"sq{r}"] = send(have[f"q{r}"], "chan", swap)
+            elif kind == "h":
+                have[f"h{r}"] = send(current, "dist", shifts[r])
+            elif kind == "k":
+                acc = stages.run([(0, 0, ((0, rounded), (1, have["sp0"])))], acc)
+            elif kind == "r":
+                acc = stages.run([(-1, r, ((0, have[f"p{r}"]), (1, have[f"q{r}"])))], acc)
+            elif kind == "s":
+                parts = [(1, r, ((1, have[f"sp{r}"]), (0, have[f"sq{r}"])))]
+                if r + 1 == far:
+                    parts.append((-1, far, ((0, have[f"p{far}"]),)))
+                acc = stages.run(parts, acc)
+            elif kind == "b":
+                sides = [have[f"h{i}"] for i in range(len(shifts))]
                 acc = stages.run([], acc, [current, before, energy, mats] + sides)
-            acc = stages.run(parts, acc)
-            p, q = next_p, next_q
-        swap_p = lax.ppermute(p, "chan", swap)
-        acc = stages.run([(RING, far, ((0, p),))], acc)
-        done = stages.run([(SWAP, far, ((1, swap_p),))], acc, out="final" if final else "both")
+            elif kind == "o":
+                kept = store(current)
+            elif kind == "e":
+                parts = [(-1, far, ((1, have[f"sp{far}"]),))]
+                done = stages.run(parts, acc, out="final" if final else "both")
         before = current
         if final:
             current = done
         else:
             current, rounded = done
-    return (current, before)
+    return (current, kept)
+
+
+def plan(far, shifts, final):
+    order = [("p", 1), ("sp", 0)] + [("h", i) for i in range(shifts)] + [("q", 1), ("k", 0)]
+    for r in range(1, far):
+        early = True
+        late = not (True)
+        order += [("p", r + 1), ("sp", r)]
+        if r > 1:
+            if late:
+                order.append(("r", r - 1))
+            order.append(("s", r - 1))
+        if r + 1 < far:
+            order.append(("q", r + 1))
+        order.append(("sq", r))
+        if r + 1 == far:
+            order.append(("b", 0))
+            order.append(("r", r))
+        elif early:
+            order.append(("r", r))
+    if final:
+        order.append(("o", 0))
+    return order + [("sp", far), ("s", far - 1), ("e", 0)]
 
 
 def solution(mesh):

time: 114 us -> 103 us (0.904)
  Pallas kernels: 32.8 us -> 20.3 us
  starting transfers between devices: 47.3 us -> 43.4 us
  waiting for transfers between devices: 31.9 us -> 35.3 us
  local copies, waits for them, and re-layouts: 1.02 us -> 2.22 us
    pallas_call x21 -> x27, Pallas kernels: 31.6 us -> 18.8 us  [run(): pl.pallas_call(kernel, out_shape=outs, in_specs=specs, out_specs=[VSPEC]...]
    ppermute x48, starting transfers between devices: 47.3 us -> 43.4 us  [send(): return lax.ppermute(x, axis, perm)]
    ppermute x48, waiting for transfers between devices: 31.9 us -> 35.3 us  [send(): return lax.ppermute(x, axis, perm)]
    unnamed x17 -> x18, local copies, waits for them, and re-layouts: 0.83 us -> 2.04 us
  transfers between devices with their start and end apart: 48 -> 48, of which waited for: 18 -> 20; matrix products, arithmetic and copies ran while one was open for 1% -> 0% of each run, Pallas kernels for 25% -> 19%
where the time goes in v1:
time: 103 us; the launch traced here: 102 us
  starting transfers between devices  43.4 us (42%)
  waiting for transfers between devices  35.3 us (34%)
  Pallas kernels  20.3 us (20%)
  local copies, waits for them, and re-layouts  2.22 us (2%)
  between operations  1.08 us (1%)
    ppermute x48, starting transfers between devices, send(): return lax.ppermute(x, axis, perm)  43.4 us
    ppermute x48, waiting for transfers between devices, send(): return lax.ppermute(x, axis, perm)  35.3 us
    pallas_call x27, Pallas kernels, run(): pl.pallas_call(kernel, out_shape=outs, in_specs=specs, out_specs=[VSPEC]...  18.8 us
  transfers between devices with their start and end apart: 48, of which 20 were waited for; matrix products, arithmetic and copies ran while one was open for 0% of the time, Pallas kernels for 19%

profile of v1, /device:TPU:0, one launch (start us, length us, event | category | flops | bytes accessed | tf_op | source)
XLA Modules:
  0.0 102.3 jit_solution(14518366453700130461)
XLA Ops:
  2.5 2.6 %collective-permute-start = (bf16[1024,128]{1,0:T(8,128)(2,1)S(1)}, bf16[1024,128]{1,0:T(8,128)(2,1)S(1)}, u32[]{:S(2)}, u32[]{:S(2)}) collective-permute-start(bf16[1024,128]{1,0:T(8,128)(2,1)S(1)} %get-tuple-element.8.refs_0_), channel_id=1, source_target_pairs={{0,8},{2,6},{8,16},{10,2},{16,24},{18,10},{24,28},{26,18},{28,20},... | collective-permute-start | bytes 786440 | tf_op jit(solution)/shard_map/ppermute | solution.py:283
  5.1 1.6 %collective-permute-start.7 = (bf16[1024,128]{1,0:T(8,128)(2,1)S(1)}, bf16[1024,128]{1,0:T(8,128)(2,1)S(1)}, u32[]{:S(2)}, u32[]{:S(2)}) collective-permute-start(bf16[1024,128]{1,0:T(8,128)(2,1)S(1)} %collective-permute-done.6.refs_1_), channel_id=1, source_target_pairs={{0,8},{2,6},{8,16},{10,2},{16,24},{18,10},{24,28},{26,18},{28,20},... | collective-permute-start | bytes 786440 | tf_op jit(solution)/shard_map/ppermute | solution.py:283
  6.7 2.7 %collective-permute-done.refs_0_ = bf16[1024,128]{1,0:T(8,128)(2,1)S(1)} collective-permute-done((bf16[1024,128]{1,0:T(8,128)(2,1)S(1)}, bf16[1024,128]{1,0:T(8,128)(2,1)S(1)}, u32[]{:S(2)}, u32[]{:S(2)}) %collective-permute-start) | collective-permute-done | bytes 262176 | tf_op jit(solution)/shard_map/ppermute | solution.py:283
  9.4 2.1 %collective-permute-start.1 = (bf16[1024,128]{1,0:T(8,128)(2,1)S(1)}, bf16[1024,128]{1,0:T(8,128)(2,1)S(1)}, u32[]{:S(2)}, u32[]{:S(2)}) collective-permute-start(bf16[1024,128]{1,0:T(8,128)(2,1)S(1)} %collective-permute-done.refs_0_), channel_id=1, source_target_pairs={{0,8},{2,6},{8,16},{10,2},{16,24},{18,10},{24,28},{26,18},{28,20},... | collective-permute-start | bytes 786440 | tf_op jit(solution)/shard_map/ppermute | solution.py:283
  12.2 2.1 %collective-permute-start.8 = (bf16[1024,128]{1,0:T(8,128)(2,1)S(1)}, bf16[1024,128]{1,0:T(8,128)(2,1)S(1)}, u32[]{:S(2)}, u32[]{:S(2)}) collective-permute-start(bf16[1024,128]{1,0:T(8,128)(2,1)S(1)} %collective-permute-done.7.refs_1_), channel_id=1, source_target_pairs={{0,8},{2,6},{8,16},{10,2},{16,24},{18,10},{24,28},{26,18},{28,20},... | collective-permute-start | bytes 786440 | tf_op jit(solution)/shard_map/ppermute | solution.py:283
  14.3 1.5 %collective-permute-done.1.refs_0_ = bf16[1024,128]{1,0:T(8,128)(2,1)S(1)} collective-permute-done((bf16[1024,128]{1,0:T(8,128)(2,1)S(1)}, bf16[1024,128]{1,0:T(8,128)(2,1)S(1)}, u32[]{:S(2)}, u32[]{:S(2)}) %collective-permute-start.1) | collective-permute-done | bytes 262176 | tf_op jit(solution)/shard_map/ppermute | solution.py:283
  15.8 2.1 %collective-permute-start.2 = (bf16[1024,128]{1,0:T(8,128)(2,1)S(1)}, bf16[1024,128]{1,0:T(8,128)(2,1)S(1)}, u32[]{:S(2)}, u32[]{:S(2)}) collective-permute-start(bf16[1024,128]{1,0:T(8,128)(2,1)S(1)} %collective-permute-done.1.refs_0_), channel_id=1, source_target_pairs={{0,8},{2,6},{8,16},{10,2},{16,24},{18,10},{24,28},{26,18},{28,20},... | collective-permute-start | bytes 786440 | tf_op jit(solution)/shard_map/ppermute | solution.py:283
  17.8 1.5 %collective-permute-start.11 = (f32[1024,128]{1,0:T(8,128)S(1)}, f32[1024,128]{1,0:T(8,128)S(1)}, u32[]{:S(2)}, u32[]{:S(2)}) collective-permute-start(f32[1024,128]{1,0:T(8,128)S(1)} %get-tuple-element.9.refs_0_.refs_1_), channel_id=1, source_target_pairs={{0,1},{1,0},{2,3},{3,2},{4,5},{5,4},{6,7},{7,6},{8,9},{9,8},{10,11... | collective-permute-start | bytes 1572872 | tf_op jit(solution)/shard_map/ppermute | solution.py:283
  19.6 1.6 %collective-permute-start.9 = (bf16[1024,128]{1,0:T(8,128)(2,1)S(1)}, bf16[1024,128]{1,0:T(8,128)(2,1)S(1)}, u32[]{:S(2)}, u32[]{:S(2)}) collective-permute-start(bf16[1024,128]{1,0:T(8,128)(2,1)S(1)} %collective-permute-done.8.refs_1_), channel_id=1, source_target_pairs={{0,8},{2,6},{8,16},{10,2},{16,24},{18,10},{24,28},{26,18},{28,20},... | collective-permute-start | bytes 786440 | tf_op jit(solution)/shard_map/ppermute | solution.py:283
  22.1 2.1 %collective-permute-start.3 = (bf16[1024,128]{1,0:T(8,128)(2,1)S(1)}, bf16[1024,128]{1,0:T(8,128)(2,1)S(1)}, u32[]{:S(2)}, u32[]{:S(2)}) collective-permute-start(bf16[1024,128]{1,0:T(8,128)(2,1)S(1)} %collective-permute-done.2.refs_0_), channel_id=1, source_target_pairs={{0,8},{2,6},{8,16},{10,2},{16,24},{18,10},{24,28},{26,18},{28,20},... | collective-permute-start | bytes 786440 | tf_op jit(solution)/shard_map/ppermute | solution.py:283
  25.9 2.8 %collective-permute-done.3.refs_2_ = bf16[1024,128]{1,0:T(8,128)(2,1)S(1)} collective-permute-done((bf16[1024,128]{1,0:T(8,128)(2,1)S(1)}, bf16[1024,128]{1,0:T(8,128)(2,1)S(1)}, u32[]{:S(2)}, u32[]{:S(2)}) %collective-permute-start.3) | collective-permute-done | bytes 262176 | tf_op jit(solution)/shard_map/ppermute | solution.py:283
  36.6 1.6 %collective-permute-start.16 = (bf16[1024,128]{1,0:T(8,128)(2,1)S(1)}, bf16[1024,128]{1,0:T(8,128)(2,1)S(1)}, u32[]{:S(2)}, u32[]{:S(2)}) collective-permute-start(bf16[1024,128]{1,0:T(8,128)(2,1)S(1)} %get-tuple-element.10.refs_0_), channel_id=1, source_target_pairs={{0,8},{2,6},{8,16},{10,2},{16,24},{18,10},{24,28},{26,18},{28,20},... | collective-permute-start | bytes 786440 | tf_op jit(solution)/shard_map/ppermute | solution.py:283
  39.7 3.4 %collective-permute-done.16.refs_0_ = bf16[1024,128]{1,0:T(8,128)(2,1)S(1)} collective-permute-done((bf16[1024,128]{1,0:T(8,128)(2,1)S(1)}, bf16[1024,128]{1,0:T(8,128)(2,1)S(1)}, u32[]{:S(2)}, u32[]{:S(2)}) %collective-permute-start.16) | collective-permute-done | bytes 262176 | tf_op jit(solution)/shard_map/ppermute | solution.py:283
  43.1 1.5 %collective-permute-start.17 = (bf16[1024,128]{1,0:T(8,128)(2,1)S(1)}, bf16[1024,128]{1,0:T(8,128)(2,1)S(1)}, u32[]{:S(2)}, u32[]{:S(2)}) collective-permute-start(bf16[1024,128]{1,0:T(8,128)(2,1)S(1)} %collective-permute-done.16.refs_0_), channel_id=1, source_target_pairs={{0,8},{2,6},{8,16},{10,2},{16,24},{18,10},{24,28},{26,18},{28,20},... | collective-permute-start | bytes 786440 | tf_op jit(solution)/shard_map/ppermute | solution.py:283
  45.9 1.5 %collective-permute-start.24 = (bf16[1024,128]{1,0:T(8,128)(2,1)S(1)}, bf16[1024,128]{1,0:T(8,128)(2,1)S(1)}, u32[]{:S(2)}, u32[]{:S(2)}) collective-permute-start(bf16[1024,128]{1,0:T(8,128)(2,1)S(1)} %collective-permute-done.23.refs_1_), channel_id=1, source_target_pairs={{0,8},{2,6},{8,16},{10,2},{16,24},{18,10},{24,28},{26,18},{28,20},... | collective-permute-start | bytes 786440 | tf_op jit(solution)/shard_map/ppermute | solution.py:283
  47.4 2.0 %collective-permute-done.17.refs_0_ = bf16[1024,128]{1,0:T(8,128)(2,1)S(1)} collective-permute-done((bf16[1024,128]{1,0:T(8,128)(2,1)S(1)}, bf16[1024,128]{1,0:T(8,128)(2,1)S(1)}, u32[]{:S(2)}, u32[]{:S(2)}) %collective-permute-start.17) | collective-permute-done | bytes 262176 | tf_op jit(solution)/shard_map/ppermute | solution.py:283
  49.4 1.5 %collective-permute-start.18 = (bf16[1024,128]{1,0:T(8,128)(2,1)S(1)}, bf16[1024,128]{1,0:T(8,128)(2,1)S(1)}, u32[]{:S(2)}, u32[]{:S(2)}) collective-permute-start(bf16[1024,128]{1,0:T(8,128)(2,1)S(1)} %collective-permute-done.17.refs_0_), channel_id=1, source_target_pairs={{0,8},{2,6},{8,16},{10,2},{16,24},{18,10},{24,28},{26,18},{28,20},... | collective-permute-start | bytes 786440 | tf_op jit(solution)/shard_map/ppermute | solution.py:283
  51.0 1.5 %collective-permute-start.27 = (f32[1024,128]{1,0:T(8,128)S(1)}, f32[1024,128]{1,0:T(8,128)S(1)}, u32[]{:S(2)}, u32[]{:S(2)}) collective-permute-start(f32[1024,128]{1,0:T(8,128)S(1)} %get-tuple-element.11.refs_0_.refs_1_), channel_id=1, source_target_pairs={{0,1},{1,0},{2,3},{3,2},{4,5},{5,4},{6,7},{7,6},{8,9},{9,8},{10,11... | collective-permute-start | bytes 1572872 | tf_op jit(solution)/shard_map/ppermute | solution.py:283
  54.2 1.6 %collective-permute-done.18.refs_0_ = bf16[1024,128]{1,0:T(8,128)(2,1)S(1)} collective-permute-done((bf16[1024,128]{1,0:T(8,128)(2,1)S(1)}, bf16[1024,128]{1,0:T(8,128)(2,1)S(1)}, u32[]{:S(2)}, u32[]{:S(2)}) %collective-permute-start.18) | collective-permute-done | bytes 262176 | tf_op jit(solution)/shard_map/ppermute | solution.py:283
  55.8 1.5 %collective-permute-start.19 = (bf16[1024,128]{1,0:T(8,128)(2,1)S(1)}, bf16[1024,128]{1,0:T(8,128)(2,1)S(1)}, u32[]{:S(2)}, u32[]{:S(2)}) collective-permute-start(bf16[1024,128]{1,0:T(8,128)(2,1)S(1)} %collective-permute-done.18.refs_0_), channel_id=1, source_target_pairs={{0,8},{2,6},{8,16},{10,2},{16,24},{18,10},{24,28},{26,18},{28,20},... | collective-permute-start | bytes 786440 | tf_op jit(solution)/shard_map/ppermute | solution.py:283
  59.1 3.1 %collective-permute-done.19.refs_2_ = bf16[1024,128]{1,0:T(8,128)(2,1)S(1)} collective-permute-done((bf16[1024,128]{1,0:T(8,128)(2,1)S(1)}, bf16[1024,128]{1,0:T(8,128)(2,1)S(1)}, u32[]{:S(2)}, u32[]{:S(2)}) %collective-permute-start.19) | collective-permute-done | bytes 262176 | tf_op jit(solution)/shard_map/ppermute | solution.py:283
  69.0 1.6 %collective-permute-start.32 = (bf16[1024,128]{1,0:T(8,128)(2,1)S(1)}, bf16[1024,128]{1,0:T(8,128)(2,1)S(1)}, u32[]{:S(2)}, u32[]{:S(2)}) collective-permute-start(bf16[1024,128]{1,0:T(8,128)(2,1)S(1)} %get-tuple-element.12.refs_0_), channel_id=1, source_target_pairs={{0,8},{2,6},{8,16},{10,2},{16,24},{18,10},{24,28},{26,18},{28,20},... | collective-permute-start | bytes 786440 | tf_op jit(solution)/shard_map/ppermute | solution.py:283
  70.6 1.6 %collective-permute-start.39 = (bf16[1024,128]{1,0:T(8,128)(2,1)S(1)}, bf16[1024,128]{1,0:T(8,128)(2,1)S(1)}, u32[]{:S(2)}, u32[]{:S(2)}) collective-permute-start(bf16[1024,128]{1,0:T(8,128)(2,1)S(1)} %collective-permute-done.38.refs_1_), channel_id=1, source_target_pairs={{0,8},{2,6},{8,16},{10,2},{16,24},{18,10},{24,28},{26,18},{28,20},... | collective-permute-start | bytes 786440 | tf_op jit(solution)/shard_map/ppermute | solution.py:283
  72.2 3.2 %collective-permute-done.32.refs_0_ = bf16[1024,128]{1,0:T(8,128)(2,1)S(1)} collective-permute-done((bf16[1024,128]{1,0:T(8,128)(2,1)S(1)}, bf16[1024,128]{1,0:T(8,128)(2,1)S(1)}, u32[]{:S(2)}, u32[]{:S(2)}) %collective-permute-start.32) | collective-permute-done | bytes 262176 | tf_op jit(solution)/shard_map/ppermute | solution.py:283
  75.4 1.6 %collective-permute-start.33 = (bf16[1024,128]{1,0:T(8,128)(2,1)S(1)}, bf16[1024,128]{1,0:T(8,128)(2,1)S(1)}, u32[]{:S(2)}, u32[]{:S(2)}) collective-permute-start(bf16[1024,128]{1,0:T(8,128)(2,1)S(1)} %collective-permute-done.32.refs_0_), channel_id=1, source_target_pairs={{0,8},{2,6},{8,16},{10,2},{16,24},{18,10},{24,28},{26,18},{28,20},... | collective-permute-start | bytes 786440 | tf_op jit(solution)/shard_map/ppermute | solution.py:283
  78.2 1.6 %collective-permute-start.40 = (bf16[1024,128]{1,0:T(8,128)(2,1)S(1)}, bf16[1024,128]{1,0:T(8,128)(2,1)S(1)}, u32[]{:S(2)}, u32[]{:S(2)}) collective-permute-start(bf16[1024,128]{1,0:T(8,128)(2,1)S(1)} %collective-permute-done.39.refs_1_), channel_id=1, source_target_pairs={{0,8},{2,6},{8,16},{10,2},{16,24},{18,10},{24,28},{26,18},{28,20},... | collective-permute-start | bytes 786440 | tf_op jit(solution)/shard_map/ppermute | solution.py:283
  79.8 2.0 %collective-permute-done.33.refs_0_ = bf16[1024,128]{1,0:T(8,128)(2,1)S(1)} collective-permute-done((bf16[1024,128]{1,0:T(8,128)(2,1)S(1)}, bf16[1024,128]{1,0:T(8,128)(2,1)S(1)}, u32[]{:S(2)}, u32[]{:S(2)}) %collective-permute-start.33) | collective-permute-done | bytes 262176 | tf_op jit(solution)/shard_map/ppermute | solution.py:283
  81.8 1.6 %collective-permute-start.34 = (bf16[1024,128]{1,0:T(8,128)(2,1)S(1)}, bf16[1024,128]{1,0:T(8,128)(2,1)S(1)}, u32[]{:S(2)}, u32[]{:S(2)}) collective-permute-start(bf16[1024,128]{1,0:T(8,128)(2,1)S(1)} %collective-permute-done.33.refs_0_), channel_id=1, source_target_pairs={{0,8},{2,6},{8,16},{10,2},{16,24},{18,10},{24,28},{26,18},{28,20},... | collective-permute-start | bytes 786440 | tf_op jit(solution)/shard_map/ppermute | solution.py:283
  83.4 1.5 %collective-permute-start.43 = (f32[1024,128]{1,0:T(8,128)S(1)}, f32[1024,128]{1,0:T(8,128)S(1)}, u32[]{:S(2)}, u32[]{:S(2)}) collective-permute-start(f32[1024,128]{1,0:T(8,128)S(1)} %get-tuple-element.13.refs_0_.x), channel_id=1, source_target_pairs={{0,1},{1,0},{2,3},{3,2},{4,5},{5,4},{6,7},{7,6},{8,9},{9,8},{10,11... | collective-permute-start | bytes 1572872 | tf_op jit(solution)/shard_map/ppermute | solution.py:283
  86.5 1.7 %collective-permute-done.34.refs_0_ = bf16[1024,128]{1,0:T(8,128)(2,1)S(1)} collective-permute-done((bf16[1024,128]{1,0:T(8,128)(2,1)S(1)}, bf16[1024,128]{1,0:T(8,128)(2,1)S(1)}, u32[]{:S(2)}, u32[]{:S(2)}) %collective-permute-start.34) | collective-permute-done | bytes 262176 | tf_op jit(solution)/shard_map/ppermute | solution.py:283
  88.1 1.6 %collective-permute-start.35 = (bf16[1024,128]{1,0:T(8,128)(2,1)S(1)}, bf16[1024,128]{1,0:T(8,128)(2,1)S(1)}, u32[]{:S(2)}, u32[]{:S(2)}) collective-permute-start(bf16[1024,128]{1,0:T(8,128)(2,1)S(1)} %collective-permute-done.34.refs_0_), channel_id=1, source_target_pairs={{0,8},{2,6},{8,16},{10,2},{16,24},{18,10},{24,28},{26,18},{28,20},... | collective-permute-start | bytes 786440 | tf_op jit(solution)/shard_map/ppermute | solution.py:283
  91.5 3.0 %collective-permute-done.35.refs_2_ = bf16[1024,128]{1,0:T(8,128)(2,1)S(1)} collective-permute-done((bf16[1024,128]{1,0:T(8,128)(2,1)S(1)}, bf16[1024,128]{1,0:T(8,128)(2,1)S(1)}, u32[]{:S(2)}, u32[]{:S(2)}) %collective-permute-start.35) | collective-permute-done | bytes 262176 | tf_op jit(solution)/shard_map/ppermute | solution.py:283
  (113 shorter events, 38.3 us)
Async XLA Ops:
  2.5 6.9 %collective-permute-start = (bf16[1024,128]{1,0:T(8,128)(2,1)S(1)}, bf16[1024,128]{1,0:T(8,128)(2,1)S(1)}, u32[]{:S(2)}, u32[]{:S(2)}) collective-permute-start(bf16[1024,128]{1,0:T(8,128)(2,1)S(1)} %get-tuple-element.8.refs_0_), channel_id=1, source_target_pairs={{0,8},{2,6},{8,16},{10,2},{16,24},{18,10},{24,28},{26,18},{28,20},... | collective-permute-start | bytes 786440 | tf_op jit(solution)/shard_map/ppermute | solution.py:283
  5.1 7.1 %collective-permute-start.7 = (bf16[1024,128]{1,0:T(8,128)(2,1)S(1)}, bf16[1024,128]{1,0:T(8,128)(2,1)S(1)}, u32[]{:S(2)}, u32[]{:S(2)}) collective-permute-start(bf16[1024,128]{1,0:T(8,128)(2,1)S(1)} %collective-permute-done.6.refs_1_), channel_id=1, source_target_pairs={{0,8},{2,6},{8,16},{10,2},{16,24},{18,10},{24,28},{26,18},{28,20},... | collective-permute-start | bytes 786440 | tf_op jit(solution)/shard_map/ppermute | solution.py:283
  11.5 7.9 %collective-permute-start.14 = (bf16[1024,128]{1,0:T(8,128)(2,1)S(1)}, bf16[1024,128]{1,0:T(8,128)(2,1)S(1)}, u32[]{:S(2)}, u32[]{:S(2)}) collective-permute-start(bf16[1024,128]{1,0:T(8,128)(2,1)S(1)} %collective-permute-done.refs_0_), channel_id=1, source_target_pairs={{0,2},{2,0},{4,6},{6,4},{8,10},{10,8},{12,14},{14,12},{16,18},{18,... | collective-permute-start | bytes 786440 | tf_op jit(solution)/shard_map/ppermute | solution.py:283
  12.2 7.4 %collective-permute-start.8 = (bf16[1024,128]{1,0:T(8,128)(2,1)S(1)}, bf16[1024,128]{1,0:T(8,128)(2,1)S(1)}, u32[]{:S(2)}, u32[]{:S(2)}) collective-permute-start(bf16[1024,128]{1,0:T(8,128)(2,1)S(1)} %collective-permute-done.7.refs_1_), channel_id=1, source_target_pairs={{0,8},{2,6},{8,16},{10,2},{16,24},{18,10},{24,28},{26,18},{28,20},... | collective-permute-start | bytes 786440 | tf_op jit(solution)/shard_map/ppermute | solution.py:283
  17.8 6.4 %collective-permute-start.15 = (bf16[1024,128]{1,0:T(8,128)(2,1)S(1)}, bf16[1024,128]{1,0:T(8,128)(2,1)S(1)}, u32[]{:S(2)}, u32[]{:S(2)}) collective-permute-start(bf16[1024,128]{1,0:T(8,128)(2,1)S(1)} %collective-permute-done.7.refs_1_), channel_id=1, source_target_pairs={{0,2},{2,0},{4,6},{6,4},{8,10},{10,8},{12,14},{14,12},{16,18},{18,... | collective-permute-start | bytes 786440 | tf_op jit(solution)/shard_map/ppermute | solution.py:283
  17.8 14.3 %collective-permute-start.11 = (f32[1024,128]{1,0:T(8,128)S(1)}, f32[1024,128]{1,0:T(8,128)S(1)}, u32[]{:S(2)}, u32[]{:S(2)}) collective-permute-start(f32[1024,128]{1,0:T(8,128)S(1)} %get-tuple-element.9.refs_0_.refs_1_), channel_id=1, source_target_pairs={{0,1},{1,0},{2,3},{3,2},{4,5},{5,4},{6,7},{7,6},{8,9},{9,8},{10,11... | collective-permute-start | bytes 1572872 | tf_op jit(solution)/shard_map/ppermute | solution.py:283
  19.6 6.4 %collective-permute-start.9 = (bf16[1024,128]{1,0:T(8,128)(2,1)S(1)}, bf16[1024,128]{1,0:T(8,128)(2,1)S(1)}, u32[]{:S(2)}, u32[]{:S(2)}) collective-permute-start(bf16[1024,128]{1,0:T(8,128)(2,1)S(1)} %collective-permute-done.8.refs_1_), channel_id=1, source_target_pairs={{0,8},{2,6},{8,16},{10,2},{16,24},{18,10},{24,28},{26,18},{28,20},... | collective-permute-start | bytes 786440 | tf_op jit(solution)/shard_map/ppermute | solution.py:283
  22.1 6.6 %collective-permute-start.3 = (bf16[1024,128]{1,0:T(8,128)(2,1)S(1)}, bf16[1024,128]{1,0:T(8,128)(2,1)S(1)}, u32[]{:S(2)}, u32[]{:S(2)}) collective-permute-start(bf16[1024,128]{1,0:T(8,128)(2,1)S(1)} %collective-permute-done.2.refs_0_), channel_id=1, source_target_pairs={{0,8},{2,6},{8,16},{10,2},{16,24},{18,10},{24,28},{26,18},{28,20},... | collective-permute-start | bytes 786440 | tf_op jit(solution)/shard_map/ppermute | solution.py:283
  24.2 7.9 %collective-permute-start.13 = (bf16[1024,128]{1,0:T(8,128)(2,1)S(1)}, bf16[1024,128]{1,0:T(8,128)(2,1)S(1)}, u32[]{:S(2)}, u32[]{:S(2)}) collective-permute-start(bf16[1024,128]{1,0:T(8,128)(2,1)S(1)} %collective-permute-done.8.refs_1_), channel_id=1, source_target_pairs={{0,2},{2,0},{4,6},{6,4},{8,10},{10,8},{12,14},{14,12},{16,18},{18,... | collective-permute-start | bytes 786440 | tf_op jit(solution)/shard_map/ppermute | solution.py:283
  24.2 10.9 %collective-permute-start.5 = (bf16[1024,128]{1,0:T(8,128)(2,1)S(1)}, bf16[1024,128]{1,0:T(8,128)(2,1)S(1)}, u32[]{:S(2)}, u32[]{:S(2)}) collective-permute-start(bf16[1024,128]{1,0:T(8,128)(2,1)S(1)} %collective-permute-done.2.refs_0_), channel_id=1, source_target_pairs={{0,2},{2,0},{4,6},{6,4},{8,10},{10,8},{12,14},{14,12},{16,18},{18,... | collective-permute-start | bytes 786440 | tf_op jit(solution)/shard_map/ppermute | solution.py:283
  25.9 9.2 %collective-permute-start.10 = (bf16[1024,128]{1,0:T(8,128)(2,1)S(1)}, bf16[1024,128]{1,0:T(8,128)(2,1)S(1)}, u32[]{:S(2)}, u32[]{:S(2)}) collective-permute-start(bf16[1024,128]{1,0:T(8,128)(2,1)S(1)} %collective-permute-done.9.refs_1_), channel_id=1, source_target_pairs={{0,2},{2,0},{4,6},{6,4},{8,10},{10,8},{12,14},{14,12},{16,18},{18,... | collective-permute-start | bytes 786440 | tf_op jit(solution)/shard_map/ppermute | solution.py:283
  28.8 7.7 %collective-permute-start.4 = (bf16[1024,128]{1,0:T(8,128)(2,1)S(1)}, bf16[1024,128]{1,0:T(8,128)(2,1)S(1)}, u32[]{:S(2)}, u32[]{:S(2)}) collective-permute-start(bf16[1024,128]{1,0:T(8,128)(2,1)S(1)} %collective-permute-done.3.refs_2_), channel_id=1, source_target_pairs={{0,2},{2,0},{4,6},{6,4},{8,10},{10,8},{12,14},{14,12},{16,18},{18,... | collective-permute-start | bytes 786440 | tf_op jit(solution)/shard_map/ppermute | solution.py:283
  36.6 6.4 %collective-permute-start.16 = (bf16[1024,128]{1,0:T(8,128)(2,1)S(1)}, bf16[1024,128]{1,0:T(8,128)(2,1)S(1)}, u32[]{:S(2)}, u32[]{:S(2)}) collective-permute-start(bf16[1024,128]{1,0:T(8,128)(2,1)S(1)} %get-tuple-element.10.refs_0_), channel_id=1, source_target_pairs={{0,8},{2,6},{8,16},{10,2},{16,24},{18,10},{24,28},{26,18},{28,20},... | collective-permute-start | bytes 786440 | tf_op jit(solution)/shard_map/ppermute | solution.py:283
  38.2 7.6 %collective-permute-start.23 = (bf16[1024,128]{1,0:T(8,128)(2,1)S(1)}, bf16[1024,128]{1,0:T(8,128)(2,1)S(1)}, u32[]{:S(2)}, u32[]{:S(2)}) collective-permute-start(bf16[1024,128]{1,0:T(8,128)(2,1)S(1)} %collective-permute-done.22.refs_1_), channel_id=1, source_target_pairs={{0,8},{2,6},{8,16},{10,2},{16,24},{18,10},{24,28},{26,18},{28,20},... | collective-permute-start | bytes 786440 | tf_op jit(solution)/shard_map/ppermute | solution.py:283
  44.6 7.9 %collective-permute-start.30 = (bf16[1024,128]{1,0:T(8,128)(2,1)S(1)}, bf16[1024,128]{1,0:T(8,128)(2,1)S(1)}, u32[]{:S(2)}, u32[]{:S(2)}) collective-permute-start(bf16[1024,128]{1,0:T(8,128)(2,1)S(1)} %collective-permute-done.16.refs_0_), channel_id=1, source_target_pairs={{0,2},{2,0},{4,6},{6,4},{8,10},{10,8},{12,14},{14,12},{16,18},{18,... | collective-permute-start | bytes 786440 | tf_op jit(solution)/shard_map/ppermute | solution.py:283
  45.9 6.8 %collective-permute-start.24 = (bf16[1024,128]{1,0:T(8,128)(2,1)S(1)}, bf16[1024,128]{1,0:T(8,128)(2,1)S(1)}, u32[]{:S(2)}, u32[]{:S(2)}) collective-permute-start(bf16[1024,128]{1,0:T(8,128)(2,1)S(1)} %collective-permute-done.23.refs_1_), channel_id=1, source_target_pairs={{0,8},{2,6},{8,16},{10,2},{16,24},{18,10},{24,28},{26,18},{28,20},... | collective-permute-start | bytes 786440 | tf_op jit(solution)/shard_map/ppermute | solution.py:283
  51.0 6.4 %collective-permute-start.31 = (bf16[1024,128]{1,0:T(8,128)(2,1)S(1)}, bf16[1024,128]{1,0:T(8,128)(2,1)S(1)}, u32[]{:S(2)}, u32[]{:S(2)}) collective-permute-start(bf16[1024,128]{1,0:T(8,128)(2,1)S(1)} %collective-permute-done.23.refs_1_), channel_id=1, source_target_pairs={{0,2},{2,0},{4,6},{6,4},{8,10},{10,8},{12,14},{14,12},{16,18},{18,... | collective-permute-start | bytes 786440 | tf_op jit(solution)/shard_map/ppermute | solution.py:283
  51.0 14.3 %collective-permute-start.27 = (f32[1024,128]{1,0:T(8,128)S(1)}, f32[1024,128]{1,0:T(8,128)S(1)}, u32[]{:S(2)}, u32[]{:S(2)}) collective-permute-start(f32[1024,128]{1,0:T(8,128)S(1)} %get-tuple-element.11.refs_0_.refs_1_), channel_id=1, source_target_pairs={{0,1},{1,0},{2,3},{3,2},{4,5},{5,4},{6,7},{7,6},{8,9},{9,8},{10,11... | collective-permute-start | bytes 1572872 | tf_op jit(solution)/shard_map/ppermute | solution.py:283
  52.7 6.4 %collective-permute-start.25 = (bf16[1024,128]{1,0:T(8,128)(2,1)S(1)}, bf16[1024,128]{1,0:T(8,128)(2,1)S(1)}, u32[]{:S(2)}, u32[]{:S(2)}) collective-permute-start(bf16[1024,128]{1,0:T(8,128)(2,1)S(1)} %collective-permute-done.24.refs_1_), channel_id=1, source_target_pairs={{0,8},{2,6},{8,16},{10,2},{16,24},{18,10},{24,28},{26,18},{28,20},... | collective-permute-start | bytes 786440 | tf_op jit(solution)/shard_map/ppermute | solution.py:283
  57.4 7.6 %collective-permute-start.29 = (bf16[1024,128]{1,0:T(8,128)(2,1)S(1)}, bf16[1024,128]{1,0:T(8,128)(2,1)S(1)}, u32[]{:S(2)}, u32[]{:S(2)}) collective-permute-start(bf16[1024,128]{1,0:T(8,128)(2,1)S(1)} %collective-permute-done.24.refs_1_), channel_id=1, source_target_pairs={{0,2},{2,0},{4,6},{6,4},{8,10},{10,8},{12,14},{14,12},{16,18},{18,... | collective-permute-start | bytes 786440 | tf_op jit(solution)/shard_map/ppermute | solution.py:283
  57.4 9.9 %collective-permute-start.21 = (bf16[1024,128]{1,0:T(8,128)(2,1)S(1)}, bf16[1024,128]{1,0:T(8,128)(2,1)S(1)}, u32[]{:S(2)}, u32[]{:S(2)}) collective-permute-start(bf16[1024,128]{1,0:T(8,128)(2,1)S(1)} %collective-permute-done.18.refs_0_), channel_id=1, source_target_pairs={{0,2},{2,0},{4,6},{6,4},{8,10},{10,8},{12,14},{14,12},{16,18},{18,... | collective-permute-start | bytes 786440 | tf_op jit(solution)/shard_map/ppermute | solution.py:283
  59.1 8.2 %collective-permute-start.26 = (bf16[1024,128]{1,0:T(8,128)(2,1)S(1)}, bf16[1024,128]{1,0:T(8,128)(2,1)S(1)}, u32[]{:S(2)}, u32[]{:S(2)}) collective-permute-start(bf16[1024,128]{1,0:T(8,128)(2,1)S(1)} %collective-permute-done.25.refs_1_), channel_id=1, source_target_pairs={{0,2},{2,0},{4,6},{6,4},{8,10},{10,8},{12,14},{14,12},{16,18},{18,... | collective-permute-start | bytes 786440 | tf_op jit(solution)/shard_map/ppermute | solution.py:283
  62.2 6.4 %collective-permute-start.20 = (bf16[1024,128]{1,0:T(8,128)(2,1)S(1)}, bf16[1024,128]{1,0:T(8,128)(2,1)S(1)}, u32[]{:S(2)}, u32[]{:S(2)}) collective-permute-start(bf16[1024,128]{1,0:T(8,128)(2,1)S(1)} %collective-permute-done.19.refs_2_), channel_id=1, source_target_pairs={{0,2},{2,0},{4,6},{6,4},{8,10},{10,8},{12,14},{14,12},{16,18},{18,... | collective-permute-start | bytes 786440 | tf_op jit(solution)/shard_map/ppermute | solution.py:283
  70.6 7.6 %collective-permute-start.39 = (bf16[1024,128]{1,0:T(8,128)(2,1)S(1)}, bf16[1024,128]{1,0:T(8,128)(2,1)S(1)}, u32[]{:S(2)}, u32[]{:S(2)}) collective-permute-start(bf16[1024,128]{1,0:T(8,128)(2,1)S(1)} %collective-permute-done.38.refs_1_), channel_id=1, source_target_pairs={{0,8},{2,6},{8,16},{10,2},{16,24},{18,10},{24,28},{26,18},{28,20},... | collective-permute-start | bytes 786440 | tf_op jit(solution)/shard_map/ppermute | solution.py:283
  77.0 7.9 %collective-permute-start.46 = (bf16[1024,128]{1,0:T(8,128)(2,1)S(1)}, bf16[1024,128]{1,0:T(8,128)(2,1)S(1)}, u32[]{:S(2)}, u32[]{:S(2)}) collective-permute-start(bf16[1024,128]{1,0:T(8,128)(2,1)S(1)} %collective-permute-done.32.refs_0_), channel_id=1, source_target_pairs={{0,2},{2,0},{4,6},{6,4},{8,10},{10,8},{12,14},{14,12},{16,18},{18,... | collective-permute-start | bytes 786440 | tf_op jit(solution)/shard_map/ppermute | solution.py:283
  78.2 6.9 %collective-permute-start.40 = (bf16[1024,128]{1,0:T(8,128)(2,1)S(1)}, bf16[1024,128]{1,0:T(8,128)(2,1)S(1)}, u32[]{:S(2)}, u32[]{:S(2)}) collective-permute-start(bf16[1024,128]{1,0:T(8,128)(2,1)S(1)} %collective-permute-done.39.refs_1_), channel_id=1, source_target_pairs={{0,8},{2,6},{8,16},{10,2},{16,24},{18,10},{24,28},{26,18},{28,20},... | collective-permute-start | bytes 786440 | tf_op jit(solution)/shard_map/ppermute | solution.py:283
  83.4 6.4 %collective-permute-start.47 = (bf16[1024,128]{1,0:T(8,128)(2,1)S(1)}, bf16[1024,128]{1,0:T(8,128)(2,1)S(1)}, u32[]{:S(2)}, u32[]{:S(2)}) collective-permute-start(bf16[1024,128]{1,0:T(8,128)(2,1)S(1)} %collective-permute-done.39.refs_1_), channel_id=1, source_target_pairs={{0,2},{2,0},{4,6},{6,4},{8,10},{10,8},{12,14},{14,12},{16,18},{18,... | collective-permute-start | bytes 786440 | tf_op jit(solution)/shard_map/ppermute | solution.py:283
  83.4 14.8 %collective-permute-start.43 = (f32[1024,128]{1,0:T(8,128)S(1)}, f32[1024,128]{1,0:T(8,128)S(1)}, u32[]{:S(2)}, u32[]{:S(2)}) collective-permute-start(f32[1024,128]{1,0:T(8,128)S(1)} %get-tuple-element.13.refs_0_.x), channel_id=1, source_target_pairs={{0,1},{1,0},{2,3},{3,2},{4,5},{5,4},{6,7},{7,6},{8,9},{9,8},{10,11... | collective-permute-start | bytes 1572872 | tf_op jit(solution)/shard_map/ppermute | solution.py:283
  89.7 8.2 %collective-permute-start.45 = (bf16[1024,128]{1,0:T(8,128)(2,1)S(1)}, bf16[1024,128]{1,0:T(8,128)(2,1)S(1)}, u32[]{:S(2)}, u32[]{:S(2)}) collective-permute-start(bf16[1024,128]{1,0:T(8,128)(2,1)S(1)} %collective-permute-done.40.refs_1_), channel_id=1, source_target_pairs={{0,2},{2,0},{4,6},{6,4},{8,10},{10,8},{12,14},{14,12},{16,18},{18,... | collective-permute-start | bytes 786440 | tf_op jit(solution)/shard_map/ppermute | solution.py:283
  89.7 10.4 %collective-permute-start.37 = (bf16[1024,128]{1,0:T(8,128)(2,1)S(1)}, bf16[1024,128]{1,0:T(8,128)(2,1)S(1)}, u32[]{:S(2)}, u32[]{:S(2)}) collective-permute-start(bf16[1024,128]{1,0:T(8,128)(2,1)S(1)} %collective-permute-done.34.refs_0_), channel_id=1, source_target_pairs={{0,2},{2,0},{4,6},{6,4},{8,10},{10,8},{12,14},{14,12},{16,18},{18,... | collective-permute-start | bytes 786440 | tf_op jit(solution)/shard_map/ppermute | solution.py:283
  91.5 8.7 %collective-permute-start.42 = (bf16[1024,128]{1,0:T(8,128)(2,1)S(1)}, bf16[1024,128]{1,0:T(8,128)(2,1)S(1)}, u32[]{:S(2)}, u32[]{:S(2)}) collective-permute-start(bf16[1024,128]{1,0:T(8,128)(2,1)S(1)} %collective-permute-done.41.refs_1_), channel_id=1, source_target_pairs={{0,2},{2,0},{4,6},{6,4},{8,10},{10,8},{12,14},{14,12},{16,18},{18,... | collective-permute-start | bytes 786440 | tf_op jit(solution)/shard_map/ppermute | solution.py:283
  94.5 6.9 %collective-permute-start.36 = (bf16[1024,128]{1,0:T(8,128)(2,1)S(1)}, bf16[1024,128]{1,0:T(8,128)(2,1)S(1)}, u32[]{:S(2)}, u32[]{:S(2)}) collective-permute-start(bf16[1024,128]{1,0:T(8,128)(2,1)S(1)} %collective-permute-done.35.refs_2_), channel_id=1, source_target_pairs={{0,2},{2,0},{4,6},{6,4},{8,10},{10,8},{12,14},{14,12},{16,18},{18,... | collective-permute-start | bytes 786440 | tf_op jit(solution)/shard_map/ppermute | solution.py:283
  (25 other events, 229.3 us)

commit v2 on v1

--- a/solution.py
+++ b/solution.py
@@ -305,10 +305,9 @@
             elif kind == "r":
                 acc = stages.run([(-1, r, ((0, have[f"p{r}"]), (1, have[f"q{r}"])))], acc)
             elif kind == "s":
-                parts = [(1, r, ((1, have[f"sp{r}"]), (0, have[f"sq{r}"])))]
-                if r + 1 == far:
-                    parts.append((-1, far, ((0, have[f"p{far}"]),)))
-                acc = stages.run(parts, acc)
+                acc = stages.run([(1, r, ((1, have[f"sp{r}"]), (0, have[f"sq{r}"])))], acc)
+            elif kind == "f":
+                acc = stages.run([(-1, r, ((0, have[f"p{r}"]),))], acc)
             elif kind == "b":
                 sides = [have[f"h{i}"] for i in range(len(shifts))]
                 acc = stages.run([], acc, [current, before, energy, mats] + sides)
@@ -345,7 +344,8 @@
             order.append(("r", r))
     if final:
         order.append(("o", 0))
-    return order + [("sp", far), ("s", far - 1), ("e", 0)]
+    order.append(("s", far - 1))
+    return order + [("sp", far), ("f", far), ("e", 0)]
 
 
 def solution(mesh):

time: 103 us -> 102 us (level)
    pallas_call x27 -> x30, Pallas kernels: 18.8 us -> 18.9 us  [run(): pl.pallas_call(kernel, out_shape=outs, in_specs=specs, out_specs=[VSPEC]...]
where the time goes in v2:
time: 102 us
  starting transfers between devices  43.4 us (43%)
  waiting for transfers between devices  35.1 us (34%)
  Pallas kernels  20.4 us (20%)
  local copies, waits for them, and re-layouts  2.22 us (2%)
  between operations  1.1 us (1%)
    ppermute x48, starting transfers between devices, send(): return lax.ppermute(x, axis, perm)  43.4 us
    ppermute x48, waiting for transfers between devices, send(): return lax.ppermute(x, axis, perm)  35.1 us
    pallas_call x30, Pallas kernels, run(): pl.pallas_call(kernel, out_shape=outs, in_specs=specs, out_specs=[VSPEC]...  18.9 us
  transfers between devices with their start and end apart: 48, of which 20 were waited for; matrix products, arithmetic and copies ran while one was open for 0% of the time, Pallas kernels for 19%

profile of v2, /device:TPU:0, one launch (start us, length us, event | category | flops | bytes accessed | tf_op | source)
XLA Modules:
  0.0 102.2 jit_solution(11973024392896637978)
XLA Ops:
  2.5 2.6 %collective-permute-start = (bf16[1024,128]{1,0:T(8,128)(2,1)S(1)}, bf16[1024,128]{1,0:T(8,128)(2,1)S(1)}, u32[]{:S(2)}, u32[]{:S(2)}) collective-permute-start(bf16[1024,128]{1,0:T(8,128)(2,1)S(1)} %get-tuple-element.8.refs_0_), channel_id=1, source_target_pairs={{0,8},{2,6},{8,16},{10,2},{16,24},{18,10},{24,28},{26,18},{28,20},... | collective-permute-start | bytes 786440 | tf_op jit(solution)/shard_map/ppermute | solution.py:283
  5.1 1.6 %collective-permute-start.7 = (bf16[1024,128]{1,0:T(8,128)(2,1)S(1)}, bf16[1024,128]{1,0:T(8,128)(2,1)S(1)}, u32[]{:S(2)}, u32[]{:S(2)}) collective-permute-start(bf16[1024,128]{1,0:T(8,128)(2,1)S(1)} %collective-permute-done.6.refs_1_), channel_id=1, source_target_pairs={{0,8},{2,6},{8,16},{10,2},{16,24},{18,10},{24,28},{26,18},{28,20},... | collective-permute-start | bytes 786440 | tf_op jit(solution)/shard_map/ppermute | solution.py:283
  6.7 2.7 %collective-permute-done.refs_0_ = bf16[1024,128]{1,0:T(8,128)(2,1)S(1)} collective-permute-done((bf16[1024,128]{1,0:T(8,128)(2,1)S(1)}, bf16[1024,128]{1,0:T(8,128)(2,1)S(1)}, u32[]{:S(2)}, u32[]{:S(2)}) %collective-permute-start) | collective-permute-done | bytes 262176 | tf_op jit(solution)/shard_map/ppermute | solution.py:283
  9.4 2.1 %collective-permute-start.1 = (bf16[1024,128]{1,0:T(8,128)(2,1)S(1)}, bf16[1024,128]{1,0:T(8,128)(2,1)S(1)}, u32[]{:S(2)}, u32[]{:S(2)}) collective-permute-start(bf16[1024,128]{1,0:T(8,128)(2,1)S(1)} %collective-permute-done.refs_0_), channel_id=1, source_target_pairs={{0,8},{2,6},{8,16},{10,2},{16,24},{18,10},{24,28},{26,18},{28,20},... | collective-permute-start | bytes 786440 | tf_op jit(solution)/shard_map/ppermute | solution.py:283
  12.2 2.1 %collective-permute-start.8 = (bf16[1024,128]{1,0:T(8,128)(2,1)S(1)}, bf16[1024,128]{1,0:T(8,128)(2,1)S(1)}, u32[]{:S(2)}, u32[]{:S(2)}) collective-permute-start(bf16[1024,128]{1,0:T(8,128)(2,1)S(1)} %collective-permute-done.7.refs_1_), channel_id=1, source_target_pairs={{0,8},{2,6},{8,16},{10,2},{16,24},{18,10},{24,28},{26,18},{28,20},... | collective-permute-start | bytes 786440 | tf_op jit(solution)/shard_map/ppermute | solution.py:283
  14.3 1.5 %collective-permute-done.1.refs_0_ = bf16[1024,128]{1,0:T(8,128)(2,1)S(1)} collective-permute-done((bf16[1024,128]{1,0:T(8,128)(2,1)S(1)}, bf16[1024,128]{1,0:T(8,128)(2,1)S(1)}, u32[]{:S(2)}, u32[]{:S(2)}) %collective-permute-start.1) | collective-permute-done | bytes 262176 | tf_op jit(solution)/shard_map/ppermute | solution.py:283
  15.8 2.1 %collective-permute-start.2 = (bf16[1024,128]{1,0:T(8,128)(2,1)S(1)}, bf16[1024,128]{1,0:T(8,128)(2,1)S(1)}, u32[]{:S(2)}, u32[]{:S(2)}) collective-permute-start(bf16[1024,128]{1,0:T(8,128)(2,1)S(1)} %collective-permute-done.1.refs_0_), channel_id=1, source_target_pairs={{0,8},{2,6},{8,16},{10,2},{16,24},{18,10},{24,28},{26,18},{28,20},... | collective-permute-start | bytes 786440 | tf_op jit(solution)/shard_map/ppermute | solution.py:283
  17.8 1.5 %collective-permute-start.11 = (f32[1024,128]{1,0:T(8,128)S(1)}, f32[1024,128]{1,0:T(8,128)S(1)}, u32[]{:S(2)}, u32[]{:S(2)}) collective-permute-start(f32[1024,128]{1,0:T(8,128)S(1)} %get-tuple-element.9.refs_0_.refs_1_), channel_id=1, source_target_pairs={{0,1},{1,0},{2,3},{3,2},{4,5},{5,4},{6,7},{7,6},{8,9},{9,8},{10,11... | collective-permute-start | bytes 1572872 | tf_op jit(solution)/shard_map/ppermute | solution.py:283
  19.6 1.6 %collective-permute-start.9 = (bf16[1024,128]{1,0:T(8,128)(2,1)S(1)}, bf16[1024,128]{1,0:T(8,128)(2,1)S(1)}, u32[]{:S(2)}, u32[]{:S(2)}) collective-permute-start(bf16[1024,128]{1,0:T(8,128)(2,1)S(1)} %collective-permute-done.8.refs_1_), channel_id=1, source_target_pairs={{0,8},{2,6},{8,16},{10,2},{16,24},{18,10},{24,28},{26,18},{28,20},... | collective-permute-start | bytes 786440 | tf_op jit(solution)/shard_map/ppermute | solution.py:283
  22.1 2.1 %collective-permute-start.3 = (bf16[1024,128]{1,0:T(8,128)(2,1)S(1)}, bf16[1024,128]{1,0:T(8,128)(2,1)S(1)}, u32[]{:S(2)}, u32[]{:S(2)}) collective-permute-start(bf16[1024,128]{1,0:T(8,128)(2,1)S(1)} %collective-permute-done.2.refs_0_), channel_id=1, source_target_pairs={{0,8},{2,6},{8,16},{10,2},{16,24},{18,10},{24,28},{26,18},{28,20},... | collective-permute-start | bytes 786440 | tf_op jit(solution)/shard_map/ppermute | solution.py:283
  25.9 2.8 %collective-permute-done.3.refs_0_ = bf16[1024,128]{1,0:T(8,128)(2,1)S(1)} collective-permute-done((bf16[1024,128]{1,0:T(8,128)(2,1)S(1)}, bf16[1024,128]{1,0:T(8,128)(2,1)S(1)}, u32[]{:S(2)}, u32[]{:S(2)}) %collective-permute-start.3) | collective-permute-done | bytes 262176 | tf_op jit(solution)/shard_map/ppermute | solution.py:283
  36.7 1.6 %collective-permute-start.16 = (bf16[1024,128]{1,0:T(8,128)(2,1)S(1)}, bf16[1024,128]{1,0:T(8,128)(2,1)S(1)}, u32[]{:S(2)}, u32[]{:S(2)}) collective-permute-start(bf16[1024,128]{1,0:T(8,128)(2,1)S(1)} %get-tuple-element.10.refs_0_), channel_id=1, source_target_pairs={{0,8},{2,6},{8,16},{10,2},{16,24},{18,10},{24,28},{26,18},{28,20},... | collective-permute-start | bytes 786440 | tf_op jit(solution)/shard_map/ppermute | solution.py:283
  39.7 3.4 %collective-permute-done.16.refs_0_ = bf16[1024,128]{1,0:T(8,128)(2,1)S(1)} collective-permute-done((bf16[1024,128]{1,0:T(8,128)(2,1)S(1)}, bf16[1024,128]{1,0:T(8,128)(2,1)S(1)}, u32[]{:S(2)}, u32[]{:S(2)}) %collective-permute-start.16) | collective-permute-done | bytes 262176 | tf_op jit(solution)/shard_map/ppermute | solution.py:283
  43.1 1.6 %collective-permute-start.17 = (bf16[1024,128]{1,0:T(8,128)(2,1)S(1)}, bf16[1024,128]{1,0:T(8,128)(2,1)S(1)}, u32[]{:S(2)}, u32[]{:S(2)}) collective-permute-start(bf16[1024,128]{1,0:T(8,128)(2,1)S(1)} %collective-permute-done.16.refs_0_), channel_id=1, source_target_pairs={{0,8},{2,6},{8,16},{10,2},{16,24},{18,10},{24,28},{26,18},{28,20},... | collective-permute-start | bytes 786440 | tf_op jit(solution)/shard_map/ppermute | solution.py:283
  45.9 1.6 %collective-permute-start.24 = (bf16[1024,128]{1,0:T(8,128)(2,1)S(1)}, bf16[1024,128]{1,0:T(8,128)(2,1)S(1)}, u32[]{:S(2)}, u32[]{:S(2)}) collective-permute-start(bf16[1024,128]{1,0:T(8,128)(2,1)S(1)} %collective-permute-done.23.refs_1_), channel_id=1, source_target_pairs={{0,8},{2,6},{8,16},{10,2},{16,24},{18,10},{24,28},{26,18},{28,20},... | collective-permute-start | bytes 786440 | tf_op jit(solution)/shard_map/ppermute | solution.py:283
  47.5 2.0 %collective-permute-done.17.refs_0_ = bf16[1024,128]{1,0:T(8,128)(2,1)S(1)} collective-permute-done((bf16[1024,128]{1,0:T(8,128)(2,1)S(1)}, bf16[1024,128]{1,0:T(8,128)(2,1)S(1)}, u32[]{:S(2)}, u32[]{:S(2)}) %collective-permute-start.17) | collective-permute-done | bytes 262176 | tf_op jit(solution)/shard_map/ppermute | solution.py:283
  49.5 1.6 %collective-permute-start.18 = (bf16[1024,128]{1,0:T(8,128)(2,1)S(1)}, bf16[1024,128]{1,0:T(8,128)(2,1)S(1)}, u32[]{:S(2)}, u32[]{:S(2)}) collective-permute-start(bf16[1024,128]{1,0:T(8,128)(2,1)S(1)} %collective-permute-done.17.refs_0_), channel_id=1, source_target_pairs={{0,8},{2,6},{8,16},{10,2},{16,24},{18,10},{24,28},{26,18},{28,20},... | collective-permute-start | bytes 786440 | tf_op jit(solution)/shard_map/ppermute | solution.py:283
  51.0 1.5 %collective-permute-start.27 = (f32[1024,128]{1,0:T(8,128)S(1)}, f32[1024,128]{1,0:T(8,128)S(1)}, u32[]{:S(2)}, u32[]{:S(2)}) collective-permute-start(f32[1024,128]{1,0:T(8,128)S(1)} %get-tuple-element.11.refs_0_.refs_1_), channel_id=1, source_target_pairs={{0,1},{1,0},{2,3},{3,2},{4,5},{5,4},{6,7},{7,6},{8,9},{9,8},{10,11... | collective-permute-start | bytes 1572872 | tf_op jit(solution)/shard_map/ppermute | solution.py:283
  54.2 1.7 %collective-permute-done.18.refs_0_ = bf16[1024,128]{1,0:T(8,128)(2,1)S(1)} collective-permute-done((bf16[1024,128]{1,0:T(8,128)(2,1)S(1)}, bf16[1024,128]{1,0:T(8,128)(2,1)S(1)}, u32[]{:S(2)}, u32[]{:S(2)}) %collective-permute-start.18) | collective-permute-done | bytes 262176 | tf_op jit(solution)/shard_map/ppermute | solution.py:283
  55.8 1.6 %collective-permute-start.19 = (bf16[1024,128]{1,0:T(8,128)(2,1)S(1)}, bf16[1024,128]{1,0:T(8,128)(2,1)S(1)}, u32[]{:S(2)}, u32[]{:S(2)}) collective-permute-start(bf16[1024,128]{1,0:T(8,128)(2,1)S(1)} %collective-permute-done.18.refs_0_), channel_id=1, source_target_pairs={{0,8},{2,6},{8,16},{10,2},{16,24},{18,10},{24,28},{26,18},{28,20},... | collective-permute-start | bytes 786440 | tf_op jit(solution)/shard_map/ppermute | solution.py:283
  59.1 3.1 %collective-permute-done.19.refs_0_ = bf16[1024,128]{1,0:T(8,128)(2,1)S(1)} collective-permute-done((bf16[1024,128]{1,0:T(8,128)(2,1)S(1)}, bf16[1024,128]{1,0:T(8,128)(2,1)S(1)}, u32[]{:S(2)}, u32[]{:S(2)}) %collective-permute-start.19) | collective-permute-done | bytes 262176 | tf_op jit(solution)/shard_map/ppermute | solution.py:283
  68.9 1.6 %collective-permute-start.32 = (bf16[1024,128]{1,0:T(8,128)(2,1)S(1)}, bf16[1024,128]{1,0:T(8,128)(2,1)S(1)}, u32[]{:S(2)}, u32[]{:S(2)}) collective-permute-start(bf16[1024,128]{1,0:T(8,128)(2,1)S(1)} %get-tuple-element.12.refs_0_), channel_id=1, source_target_pairs={{0,8},{2,6},{8,16},{10,2},{16,24},{18,10},{24,28},{26,18},{28,20},... | collective-permute-start | bytes 786440 | tf_op jit(solution)/shard_map/ppermute | solution.py:283
  70.5 1.7 %collective-permute-start.39 = (bf16[1024,128]{1,0:T(8,128)(2,1)S(1)}, bf16[1024,128]{1,0:T(8,128)(2,1)S(1)}, u32[]{:S(2)}, u32[]{:S(2)}) collective-permute-start(bf16[1024,128]{1,0:T(8,128)(2,1)S(1)} %collective-permute-done.38.refs_1_), channel_id=1, source_target_pairs={{0,8},{2,6},{8,16},{10,2},{16,24},{18,10},{24,28},{26,18},{28,20},... | collective-permute-start | bytes 786440 | tf_op jit(solution)/shard_map/ppermute | solution.py:283
  72.2 3.1 %collective-permute-done.32.refs_0_ = bf16[1024,128]{1,0:T(8,128)(2,1)S(1)} collective-permute-done((bf16[1024,128]{1,0:T(8,128)(2,1)S(1)}, bf16[1024,128]{1,0:T(8,128)(2,1)S(1)}, u32[]{:S(2)}, u32[]{:S(2)}) %collective-permute-start.32) | collective-permute-done | bytes 262176 | tf_op jit(solution)/shard_map/ppermute | solution.py:283
  75.3 1.6 %collective-permute-start.33 = (bf16[1024,128]{1,0:T(8,128)(2,1)S(1)}, bf16[1024,128]{1,0:T(8,128)(2,1)S(1)}, u32[]{:S(2)}, u32[]{:S(2)}) collective-permute-start(bf16[1024,128]{1,0:T(8,128)(2,1)S(1)} %collective-permute-done.32.refs_0_), channel_id=1, source_target_pairs={{0,8},{2,6},{8,16},{10,2},{16,24},{18,10},{24,28},{26,18},{28,20},... | collective-permute-start | bytes 786440 | tf_op jit(solution)/shard_map/ppermute | solution.py:283
  78.1 1.6 %collective-permute-start.40 = (bf16[1024,128]{1,0:T(8,128)(2,1)S(1)}, bf16[1024,128]{1,0:T(8,128)(2,1)S(1)}, u32[]{:S(2)}, u32[]{:S(2)}) collective-permute-start(bf16[1024,128]{1,0:T(8,128)(2,1)S(1)} %collective-permute-done.39.refs_1_), channel_id=1, source_target_pairs={{0,8},{2,6},{8,16},{10,2},{16,24},{18,10},{24,28},{26,18},{28,20},... | collective-permute-start | bytes 786440 | tf_op jit(solution)/shard_map/ppermute | solution.py:283
  79.7 2.0 %collective-permute-done.33.refs_0_ = bf16[1024,128]{1,0:T(8,128)(2,1)S(1)} collective-permute-done((bf16[1024,128]{1,0:T(8,128)(2,1)S(1)}, bf16[1024,128]{1,0:T(8,128)(2,1)S(1)}, u32[]{:S(2)}, u32[]{:S(2)}) %collective-permute-start.33) | collective-permute-done | bytes 262176 | tf_op jit(solution)/shard_map/ppermute | solution.py:283
  81.6 1.6 %collective-permute-start.34 = (bf16[1024,128]{1,0:T(8,128)(2,1)S(1)}, bf16[1024,128]{1,0:T(8,128)(2,1)S(1)}, u32[]{:S(2)}, u32[]{:S(2)}) collective-permute-start(bf16[1024,128]{1,0:T(8,128)(2,1)S(1)} %collective-permute-done.33.refs_0_), channel_id=1, source_target_pairs={{0,8},{2,6},{8,16},{10,2},{16,24},{18,10},{24,28},{26,18},{28,20},... | collective-permute-start | bytes 786440 | tf_op jit(solution)/shard_map/ppermute | solution.py:283
  83.2 1.5 %collective-permute-start.43 = (f32[1024,128]{1,0:T(8,128)S(1)}, f32[1024,128]{1,0:T(8,128)S(1)}, u32[]{:S(2)}, u32[]{:S(2)}) collective-permute-start(f32[1024,128]{1,0:T(8,128)S(1)} %get-tuple-element.13.refs_0_.x), channel_id=1, source_target_pairs={{0,1},{1,0},{2,3},{3,2},{4,5},{5,4},{6,7},{7,6},{8,9},{9,8},{10,11... | collective-permute-start | bytes 1572872 | tf_op jit(solution)/shard_map/ppermute | solution.py:283
  86.5 1.6 %collective-permute-done.34.refs_0_ = bf16[1024,128]{1,0:T(8,128)(2,1)S(1)} collective-permute-done((bf16[1024,128]{1,0:T(8,128)(2,1)S(1)}, bf16[1024,128]{1,0:T(8,128)(2,1)S(1)}, u32[]{:S(2)}, u32[]{:S(2)}) %collective-permute-start.34) | collective-permute-done | bytes 262176 | tf_op jit(solution)/shard_map/ppermute | solution.py:283
  88.0 1.6 %collective-permute-start.35 = (bf16[1024,128]{1,0:T(8,128)(2,1)S(1)}, bf16[1024,128]{1,0:T(8,128)(2,1)S(1)}, u32[]{:S(2)}, u32[]{:S(2)}) collective-permute-start(bf16[1024,128]{1,0:T(8,128)(2,1)S(1)} %collective-permute-done.34.refs_0_), channel_id=1, source_target_pairs={{0,8},{2,6},{8,16},{10,2},{16,24},{18,10},{24,28},{26,18},{28,20},... | collective-permute-start | bytes 786440 | tf_op jit(solution)/shard_map/ppermute | solution.py:283
  91.4 3.0 %collective-permute-done.35.refs_0_ = bf16[1024,128]{1,0:T(8,128)(2,1)S(1)} collective-permute-done((bf16[1024,128]{1,0:T(8,128)(2,1)S(1)}, bf16[1024,128]{1,0:T(8,128)(2,1)S(1)}, u32[]{:S(2)}, u32[]{:S(2)}) %collective-permute-start.35) | collective-permute-done | bytes 262176 | tf_op jit(solution)/shard_map/ppermute | solution.py:283
  (116 shorter events, 38.2 us)
Async XLA Ops:
  2.5 6.9 %collective-permute-start = (bf16[1024,128]{1,0:T(8,128)(2,1)S(1)}, bf16[1024,128]{1,0:T(8,128)(2,1)S(1)}, u32[]{:S(2)}, u32[]{:S(2)}) collective-permute-start(bf16[1024,128]{1,0:T(8,128)(2,1)S(1)} %get-tuple-element.8.refs_0_), channel_id=1, source_target_pairs={{0,8},{2,6},{8,16},{10,2},{16,24},{18,10},{24,28},{26,18},{28,20},... | collective-permute-start | bytes 786440 | tf_op jit(solution)/shard_map/ppermute | solution.py:283
  5.1 7.1 %collective-permute-start.7 = (bf16[1024,128]{1,0:T(8,128)(2,1)S(1)}, bf16[1024,128]{1,0:T(8,128)(2,1)S(1)}, u32[]{:S(2)}, u32[]{:S(2)}) collective-permute-start(bf16[1024,128]{1,0:T(8,128)(2,1)S(1)} %collective-permute-done.6.refs_1_), channel_id=1, source_target_pairs={{0,8},{2,6},{8,16},{10,2},{16,24},{18,10},{24,28},{26,18},{28,20},... | collective-permute-start | bytes 786440 | tf_op jit(solution)/shard_map/ppermute | solution.py:283
  11.5 7.9 %collective-permute-start.14 = (bf16[1024,128]{1,0:T(8,128)(2,1)S(1)}, bf16[1024,128]{1,0:T(8,128)(2,1)S(1)}, u32[]{:S(2)}, u32[]{:S(2)}) collective-permute-start(bf16[1024,128]{1,0:T(8,128)(2,1)S(1)} %collective-permute-done.refs_0_), channel_id=1, source_target_pairs={{0,2},{2,0},{4,6},{6,4},{8,10},{10,8},{12,14},{14,12},{16,18},{18,... | collective-permute-start | bytes 786440 | tf_op jit(solution)/shard_map/ppermute | solution.py:283
  12.2 7.4 %collective-permute-start.8 = (bf16[1024,128]{1,0:T(8,128)(2,1)S(1)}, bf16[1024,128]{1,0:T(8,128)(2,1)S(1)}, u32[]{:S(2)}, u32[]{:S(2)}) collective-permute-start(bf16[1024,128]{1,0:T(8,128)(2,1)S(1)} %collective-permute-done.7.refs_1_), channel_id=1, source_target_pairs={{0,8},{2,6},{8,16},{10,2},{16,24},{18,10},{24,28},{26,18},{28,20},... | collective-permute-start | bytes 786440 | tf_op jit(solution)/shard_map/ppermute | solution.py:283
  17.8 6.4 %collective-permute-start.15 = (bf16[1024,128]{1,0:T(8,128)(2,1)S(1)}, bf16[1024,128]{1,0:T(8,128)(2,1)S(1)}, u32[]{:S(2)}, u32[]{:S(2)}) collective-permute-start(bf16[1024,128]{1,0:T(8,128)(2,1)S(1)} %collective-permute-done.7.refs_1_), channel_id=1, source_target_pairs={{0,2},{2,0},{4,6},{6,4},{8,10},{10,8},{12,14},{14,12},{16,18},{18,... | collective-permute-start | bytes 786440 | tf_op jit(solution)/shard_map/ppermute | solution.py:283
  17.8 14.3 %collective-permute-start.11 = (f32[1024,128]{1,0:T(8,128)S(1)}, f32[1024,128]{1,0:T(8,128)S(1)}, u32[]{:S(2)}, u32[]{:S(2)}) collective-permute-start(f32[1024,128]{1,0:T(8,128)S(1)} %get-tuple-element.9.refs_0_.refs_1_), channel_id=1, source_target_pairs={{0,1},{1,0},{2,3},{3,2},{4,5},{5,4},{6,7},{7,6},{8,9},{9,8},{10,11... | collective-permute-start | bytes 1572872 | tf_op jit(solution)/shard_map/ppermute | solution.py:283
  19.6 6.4 %collective-permute-start.9 = (bf16[1024,128]{1,0:T(8,128)(2,1)S(1)}, bf16[1024,128]{1,0:T(8,128)(2,1)S(1)}, u32[]{:S(2)}, u32[]{:S(2)}) collective-permute-start(bf16[1024,128]{1,0:T(8,128)(2,1)S(1)} %collective-permute-done.8.refs_1_), channel_id=1, source_target_pairs={{0,8},{2,6},{8,16},{10,2},{16,24},{18,10},{24,28},{26,18},{28,20},... | collective-permute-start | bytes 786440 | tf_op jit(solution)/shard_map/ppermute | solution.py:283
  22.1 6.6 %collective-permute-start.3 = (bf16[1024,128]{1,0:T(8,128)(2,1)S(1)}, bf16[1024,128]{1,0:T(8,128)(2,1)S(1)}, u32[]{:S(2)}, u32[]{:S(2)}) collective-permute-start(bf16[1024,128]{1,0:T(8,128)(2,1)S(1)} %collective-permute-done.2.refs_0_), channel_id=1, source_target_pairs={{0,8},{2,6},{8,16},{10,2},{16,24},{18,10},{24,28},{26,18},{28,20},... | collective-permute-start | bytes 786440 | tf_op jit(solution)/shard_map/ppermute | solution.py:283
  24.2 7.9 %collective-permute-start.13 = (bf16[1024,128]{1,0:T(8,128)(2,1)S(1)}, bf16[1024,128]{1,0:T(8,128)(2,1)S(1)}, u32[]{:S(2)}, u32[]{:S(2)}) collective-permute-start(bf16[1024,128]{1,0:T(8,128)(2,1)S(1)} %collective-permute-done.8.refs_1_), channel_id=1, source_target_pairs={{0,2},{2,0},{4,6},{6,4},{8,10},{10,8},{12,14},{14,12},{16,18},{18,... | collective-permute-start | bytes 786440 | tf_op jit(solution)/shard_map/ppermute | solution.py:283
  24.2 10.9 %collective-permute-start.5 = (bf16[1024,128]{1,0:T(8,128)(2,1)S(1)}, bf16[1024,128]{1,0:T(8,128)(2,1)S(1)}, u32[]{:S(2)}, u32[]{:S(2)}) collective-permute-start(bf16[1024,128]{1,0:T(8,128)(2,1)S(1)} %collective-permute-done.2.refs_0_), channel_id=1, source_target_pairs={{0,2},{2,0},{4,6},{6,4},{8,10},{10,8},{12,14},{14,12},{16,18},{18,... | collective-permute-start | bytes 786440 | tf_op jit(solution)/shard_map/ppermute | solution.py:283
  25.9 9.2 %collective-permute-start.10 = (bf16[1024,128]{1,0:T(8,128)(2,1)S(1)}, bf16[1024,128]{1,0:T(8,128)(2,1)S(1)}, u32[]{:S(2)}, u32[]{:S(2)}) collective-permute-start(bf16[1024,128]{1,0:T(8,128)(2,1)S(1)} %collective-permute-done.9.refs_1_), channel_id=1, source_target_pairs={{0,2},{2,0},{4,6},{6,4},{8,10},{10,8},{12,14},{14,12},{16,18},{18,... | collective-permute-start | bytes 786440 | tf_op jit(solution)/shard_map/ppermute | solution.py:283
  28.8 7.7 %collective-permute-start.4 = (bf16[1024,128]{1,0:T(8,128)(2,1)S(1)}, bf16[1024,128]{1,0:T(8,128)(2,1)S(1)}, u32[]{:S(2)}, u32[]{:S(2)}) collective-permute-start(bf16[1024,128]{1,0:T(8,128)(2,1)S(1)} %collective-permute-done.3.refs_0_), channel_id=1, source_target_pairs={{0,2},{2,0},{4,6},{6,4},{8,10},{10,8},{12,14},{14,12},{16,18},{18,... | collective-permute-start | bytes 786440 | tf_op jit(solution)/shard_map/ppermute | solution.py:283
  36.7 6.4 %collective-permute-start.16 = (bf16[1024,128]{1,0:T(8,128)(2,1)S(1)}, bf16[1024,128]{1,0:T(8,128)(2,1)S(1)}, u32[]{:S(2)}, u32[]{:S(2)}) collective-permute-start(bf16[1024,128]{1,0:T(8,128)(2,1)S(1)} %get-tuple-element.10.refs_0_), channel_id=1, source_target_pairs={{0,8},{2,6},{8,16},{10,2},{16,24},{18,10},{24,28},{26,18},{28,20},... | collective-permute-start | bytes 786440 | tf_op jit(solution)/shard_map/ppermute | solution.py:283
  38.3 7.6 %collective-permute-start.23 = (bf16[1024,128]{1,0:T(8,128)(2,1)S(1)}, bf16[1024,128]{1,0:T(8,128)(2,1)S(1)}, u32[]{:S(2)}, u32[]{:S(2)}) collective-permute-start(bf16[1024,128]{1,0:T(8,128)(2,1)S(1)} %collective-permute-done.22.refs_1_), channel_id=1, source_target_pairs={{0,8},{2,6},{8,16},{10,2},{16,24},{18,10},{24,28},{26,18},{28,20},... | collective-permute-start | bytes 786440 | tf_op jit(solution)/shard_map/ppermute | solution.py:283
  44.6 7.9 %collective-permute-start.30 = (bf16[1024,128]{1,0:T(8,128)(2,1)S(1)}, bf16[1024,128]{1,0:T(8,128)(2,1)S(1)}, u32[]{:S(2)}, u32[]{:S(2)}) collective-permute-start(bf16[1024,128]{1,0:T(8,128)(2,1)S(1)} %collective-permute-done.16.refs_0_), channel_id=1, source_target_pairs={{0,2},{2,0},{4,6},{6,4},{8,10},{10,8},{12,14},{14,12},{16,18},{18,... | collective-permute-start | bytes 786440 | tf_op jit(solution)/shard_map/ppermute | solution.py:283
  45.9 6.9 %collective-permute-start.24 = (bf16[1024,128]{1,0:T(8,128)(2,1)S(1)}, bf16[1024,128]{1,0:T(8,128)(2,1)S(1)}, u32[]{:S(2)}, u32[]{:S(2)}) collective-permute-start(bf16[1024,128]{1,0:T(8,128)(2,1)S(1)} %collective-permute-done.23.refs_1_), channel_id=1, source_target_pairs={{0,8},{2,6},{8,16},{10,2},{16,24},{18,10},{24,28},{26,18},{28,20},... | collective-permute-start | bytes 786440 | tf_op jit(solution)/shard_map/ppermute | solution.py:283
  51.0 6.4 %collective-permute-start.31 = (bf16[1024,128]{1,0:T(8,128)(2,1)S(1)}, bf16[1024,128]{1,0:T(8,128)(2,1)S(1)}, u32[]{:S(2)}, u32[]{:S(2)}) collective-permute-start(bf16[1024,128]{1,0:T(8,128)(2,1)S(1)} %collective-permute-done.23.refs_1_), channel_id=1, source_target_pairs={{0,2},{2,0},{4,6},{6,4},{8,10},{10,8},{12,14},{14,12},{16,18},{18,... | collective-permute-start | bytes 786440 | tf_op jit(solution)/shard_map/ppermute | solution.py:283
  51.0 14.3 %collective-permute-start.27 = (f32[1024,128]{1,0:T(8,128)S(1)}, f32[1024,128]{1,0:T(8,128)S(1)}, u32[]{:S(2)}, u32[]{:S(2)}) collective-permute-start(f32[1024,128]{1,0:T(8,128)S(1)} %get-tuple-element.11.refs_0_.refs_1_), channel_id=1, source_target_pairs={{0,1},{1,0},{2,3},{3,2},{4,5},{5,4},{6,7},{7,6},{8,9},{9,8},{10,11... | collective-permute-start | bytes 1572872 | tf_op jit(solution)/shard_map/ppermute | solution.py:283
  57.4 7.6 %collective-permute-start.29 = (bf16[1024,128]{1,0:T(8,128)(2,1)S(1)}, bf16[1024,128]{1,0:T(8,128)(2,1)S(1)}, u32[]{:S(2)}, u32[]{:S(2)}) collective-permute-start(bf16[1024,128]{1,0:T(8,128)(2,1)S(1)} %collective-permute-done.24.refs_1_), channel_id=1, source_target_pairs={{0,2},{2,0},{4,6},{6,4},{8,10},{10,8},{12,14},{14,12},{16,18},{18,... | collective-permute-start | bytes 786440 | tf_op jit(solution)/shard_map/ppermute | solution.py:283
  57.4 9.9 %collective-permute-start.21 = (bf16[1024,128]{1,0:T(8,128)(2,1)S(1)}, bf16[1024,128]{1,0:T(8,128)(2,1)S(1)}, u32[]{:S(2)}, u32[]{:S(2)}) collective-permute-start(bf16[1024,128]{1,0:T(8,128)(2,1)S(1)} %collective-permute-done.18.refs_0_), channel_id=1, source_target_pairs={{0,2},{2,0},{4,6},{6,4},{8,10},{10,8},{12,14},{14,12},{16,18},{18,... | collective-permute-start | bytes 786440 | tf_op jit(solution)/shard_map/ppermute | solution.py:283
  59.1 8.2 %collective-permute-start.26 = (bf16[1024,128]{1,0:T(8,128)(2,1)S(1)}, bf16[1024,128]{1,0:T(8,128)(2,1)S(1)}, u32[]{:S(2)}, u32[]{:S(2)}) collective-permute-start(bf16[1024,128]{1,0:T(8,128)(2,1)S(1)} %collective-permute-done.25.refs_1_), channel_id=1, source_target_pairs={{0,2},{2,0},{4,6},{6,4},{8,10},{10,8},{12,14},{14,12},{16,18},{18,... | collective-permute-start | bytes 786440 | tf_op jit(solution)/shard_map/ppermute | solution.py:283
  62.2 6.4 %collective-permute-start.20 = (bf16[1024,128]{1,0:T(8,128)(2,1)S(1)}, bf16[1024,128]{1,0:T(8,128)(2,1)S(1)}, u32[]{:S(2)}, u32[]{:S(2)}) collective-permute-start(bf16[1024,128]{1,0:T(8,128)(2,1)S(1)} %collective-permute-done.19.refs_0_), channel_id=1, source_target_pairs={{0,2},{2,0},{4,6},{6,4},{8,10},{10,8},{12,14},{14,12},{16,18},{18,... | collective-permute-start | bytes 786440 | tf_op jit(solution)/shard_map/ppermute | solution.py:283
  68.9 6.4 %collective-permute-start.32 = (bf16[1024,128]{1,0:T(8,128)(2,1)S(1)}, bf16[1024,128]{1,0:T(8,128)(2,1)S(1)}, u32[]{:S(2)}, u32[]{:S(2)}) collective-permute-start(bf16[1024,128]{1,0:T(8,128)(2,1)S(1)} %get-tuple-element.12.refs_0_), channel_id=1, source_target_pairs={{0,8},{2,6},{8,16},{10,2},{16,24},{18,10},{24,28},{26,18},{28,20},... | collective-permute-start | bytes 786440 | tf_op jit(solution)/shard_map/ppermute | solution.py:283
  70.5 7.6 %collective-permute-start.39 = (bf16[1024,128]{1,0:T(8,128)(2,1)S(1)}, bf16[1024,128]{1,0:T(8,128)(2,1)S(1)}, u32[]{:S(2)}, u32[]{:S(2)}) collective-permute-start(bf16[1024,128]{1,0:T(8,128)(2,1)S(1)} %collective-permute-done.38.refs_1_), channel_id=1, source_target_pairs={{0,8},{2,6},{8,16},{10,2},{16,24},{18,10},{24,28},{26,18},{28,20},... | collective-permute-start | bytes 786440 | tf_op jit(solution)/shard_map/ppermute | solution.py:283
  76.9 7.9 %collective-permute-start.46 = (bf16[1024,128]{1,0:T(8,128)(2,1)S(1)}, bf16[1024,128]{1,0:T(8,128)(2,1)S(1)}, u32[]{:S(2)}, u32[]{:S(2)}) collective-permute-start(bf16[1024,128]{1,0:T(8,128)(2,1)S(1)} %collective-permute-done.32.refs_0_), channel_id=1, source_target_pairs={{0,2},{2,0},{4,6},{6,4},{8,10},{10,8},{12,14},{14,12},{16,18},{18,... | collective-permute-start | bytes 786440 | tf_op jit(solution)/shard_map/ppermute | solution.py:283
  78.1 6.9 %collective-permute-start.40 = (bf16[1024,128]{1,0:T(8,128)(2,1)S(1)}, bf16[1024,128]{1,0:T(8,128)(2,1)S(1)}, u32[]{:S(2)}, u32[]{:S(2)}) collective-permute-start(bf16[1024,128]{1,0:T(8,128)(2,1)S(1)} %collective-permute-done.39.refs_1_), channel_id=1, source_target_pairs={{0,8},{2,6},{8,16},{10,2},{16,24},{18,10},{24,28},{26,18},{28,20},... | collective-permute-start | bytes 786440 | tf_op jit(solution)/shard_map/ppermute | solution.py:283
  83.2 6.4 %collective-permute-start.47 = (bf16[1024,128]{1,0:T(8,128)(2,1)S(1)}, bf16[1024,128]{1,0:T(8,128)(2,1)S(1)}, u32[]{:S(2)}, u32[]{:S(2)}) collective-permute-start(bf16[1024,128]{1,0:T(8,128)(2,1)S(1)} %collective-permute-done.39.refs_1_), channel_id=1, source_target_pairs={{0,2},{2,0},{4,6},{6,4},{8,10},{10,8},{12,14},{14,12},{16,18},{18,... | collective-permute-start | bytes 786440 | tf_op jit(solution)/shard_map/ppermute | solution.py:283
  83.2 14.8 %collective-permute-start.43 = (f32[1024,128]{1,0:T(8,128)S(1)}, f32[1024,128]{1,0:T(8,128)S(1)}, u32[]{:S(2)}, u32[]{:S(2)}) collective-permute-start(f32[1024,128]{1,0:T(8,128)S(1)} %get-tuple-element.13.refs_0_.x), channel_id=1, source_target_pairs={{0,1},{1,0},{2,3},{3,2},{4,5},{5,4},{6,7},{7,6},{8,9},{9,8},{10,11... | collective-permute-start | bytes 1572872 | tf_op jit(solution)/shard_map/ppermute | solution.py:283
  89.6 8.2 %collective-permute-start.45 = (bf16[1024,128]{1,0:T(8,128)(2,1)S(1)}, bf16[1024,128]{1,0:T(8,128)(2,1)S(1)}, u32[]{:S(2)}, u32[]{:S(2)}) collective-permute-start(bf16[1024,128]{1,0:T(8,128)(2,1)S(1)} %collective-permute-done.40.refs_1_), channel_id=1, source_target_pairs={{0,2},{2,0},{4,6},{6,4},{8,10},{10,8},{12,14},{14,12},{16,18},{18,... | collective-permute-start | bytes 786440 | tf_op jit(solution)/shard_map/ppermute | solution.py:283
  89.6 10.4 %collective-permute-start.37 = (bf16[1024,128]{1,0:T(8,128)(2,1)S(1)}, bf16[1024,128]{1,0:T(8,128)(2,1)S(1)}, u32[]{:S(2)}, u32[]{:S(2)}) collective-permute-start(bf16[1024,128]{1,0:T(8,128)(2,1)S(1)} %collective-permute-done.34.refs_0_), channel_id=1, source_target_pairs={{0,2},{2,0},{4,6},{6,4},{8,10},{10,8},{12,14},{14,12},{16,18},{18,... | collective-permute-start | bytes 786440 | tf_op jit(solution)/shard_map/ppermute | solution.py:283
  91.4 8.7 %collective-permute-start.42 = (bf16[1024,128]{1,0:T(8,128)(2,1)S(1)}, bf16[1024,128]{1,0:T(8,128)(2,1)S(1)}, u32[]{:S(2)}, u32[]{:S(2)}) collective-permute-start(bf16[1024,128]{1,0:T(8,128)(2,1)S(1)} %collective-permute-done.41.refs_1_), channel_id=1, source_target_pairs={{0,2},{2,0},{4,6},{6,4},{8,10},{10,8},{12,14},{14,12},{16,18},{18,... | collective-permute-start | bytes 786440 | tf_op jit(solution)/shard_map/ppermute | solution.py:283
  94.4 7.0 %collective-permute-start.36 = (bf16[1024,128]{1,0:T(8,128)(2,1)S(1)}, bf16[1024,128]{1,0:T(8,128)(2,1)S(1)}, u32[]{:S(2)}, u32[]{:S(2)}) collective-permute-start(bf16[1024,128]{1,0:T(8,128)(2,1)S(1)} %collective-permute-done.35.refs_0_), channel_id=1, source_target_pairs={{0,2},{2,0},{4,6},{6,4},{8,10},{10,8},{12,14},{14,12},{16,18},{18,... | collective-permute-start | bytes 786440 | tf_op jit(solution)/shard_map/ppermute | solution.py:283
  (25 other events, 229.1 us)
